TPU v7x, 1024 devices: a whole 4x8x16 slice. The times are simulated.
1024 devices in a mesh: dp: 64 (over y, x, core), tensor: 16 (over z).
Axes of the slice: x: 4, y: 8, z: 16, core: 2. Of those that a mesh axis runs over, the one named last changes fastest.
Arguments:
- token_ids: int32 [32768], P('dp'), may hold values from 0 to 511
- table: bfloat16 [512, 2560], replicated, may hold values from -729 to 729
- weights: bfloat16 [2560, 10240], P(None, 'tensor'), may hold values from -6 to 6
- targets: bfloat16 [32768, 10240], P('dp', 'tensor'), may hold values from -5.5 to 5.5
- momentum: float32 [2560, 10240], P('dp', 'tensor'), may hold values from -6 to 6
Outputs:
- new_weights: bfloat16 [2560, 10240], P(None, 'tensor')
- new_momentum: float32 [2560, 10240], P('dp', 'tensor')
All inputs are finite; a program needn't handle non-finite values.
Results may differ from a plain program's by a relative error of at most 0.0052.
Values may be sent and summed in bfloat16 or wider, within the bound.
No kernel may reach another device: no remote copies, remote signals or barrier semaphores. Data moves between devices by JAX's collectives and lax.ppermute only.
A program may use at most 64 MiB of HBM per device.

v0:
```python
import jax
import jax.numpy as jnp
from jax import lax
from jax.sharding import PartitionSpec as P

epsilon = 1e-06
momentum_decay = 0.9
learning_rate = 0.25


def from_partner(value, axis, stride):
    mask = 2**stride
    pairs = [(source, source ^ mask) for source in range(lax.axis_size(axis))]
    return lax.ppermute(value, axis, pairs)


def gelu_tanh(values):
    return jax.nn.gelu(values, approximate=True)


def body(token_ids, table, weights, targets, momentum):
    rows_in = jnp.take(table, token_ids, axis=0)
    preact = jnp.dot(rows_in, weights, preferred_element_type=jnp.float32)
    activated, pullback = jax.vjp(gelu_tanh, preact)
    grad_pre = pullback(activated - targets.astype(jnp.float32))[0].astype(jnp.bfloat16)
    current = lax.dot_general(
        rows_in, grad_pre, (((0,), (0,)), ((), ())), preferred_element_type=jnp.float32
    ).astype(jnp.bfloat16)
    replicas = lax.axis_size("dp")
    tree_depth = replicas.bit_length() - 1
    replica_index = lax.axis_index("dp")
    for tree_level in range(tree_depth):
        pair_bit = tree_depth - 1 - tree_level
        upper_side = replica_index >> pair_bit & 1 == 1
        half_rows = current.shape[0] // 2
        lower_part = current[:half_rows]
        upper_part = current[half_rows:]
        kept_part = jnp.where(upper_side, upper_part, lower_part)
        sent_part = jnp.where(upper_side, lower_part, upper_part)
        received = from_partner(sent_part, "dp", pair_bit)
        own_half = kept_part.astype(jnp.float32)
        peer_half = received.astype(jnp.float32)
        first_vec = jnp.where(upper_side, peer_half, own_half)
        second_vec = jnp.where(upper_side, own_half, peer_half)
        partials = jnp.stack(
            [
                jnp.sum(first_vec * second_vec),
                jnp.sum(first_vec * first_vec),
                jnp.sum(second_vec * second_vec),
            ]
        )
        partials = lax.psum(partials, "tensor")
        for sub_level in range(tree_level + 1):
            partials = partials + from_partner(partials, "dp", tree_depth - 1 - sub_level)
        cross_dot = partials[0]
        first_sq = partials[1]
        second_sq = partials[2]
        combined = (1.0 - cross_dot / (2.0 * (first_sq + epsilon))) * first_vec + (
            1.0 - cross_dot / (2.0 * (second_sq + epsilon))
        ) * second_vec
        if tree_level + 1 < tree_depth:
            current = combined.astype(jnp.bfloat16)
        else:
            current = combined
    new_momentum = momentum_decay * momentum + current
    owned_rows = momentum.shape[0]
    own_weights = lax.dynamic_slice_in_dim(weights, replica_index * owned_rows, owned_rows, 0)
    new_piece = (own_weights.astype(jnp.float32) - learning_rate * new_momentum).astype(
        jnp.bfloat16
    )
    new_weights = lax.all_gather(new_piece, "dp", axis=0, tiled=True)
    return (new_weights, new_momentum)


def solution(mesh):
    placed = (P("dp"), P(), P(None, "tensor"), P("dp", "tensor"), P("dp", "tensor"))
    return jax.shard_map(
        body,
        mesh=mesh,
        in_specs=placed,
        out_specs=(P(None, "tensor"), P("dp", "tensor")),
        check_vma=False,
    )
```

profile of v0, /device:TPU:1, one launch (start us, length us, event | category | flops | bytes accessed | tf_op | source)
XLA Modules:
  0.0 647.9 jit_solution(1535333261051487150)
XLA Ops:
  8.9 3.5 gather_fusion
  12.4 10.0 %convolution_convert_fusion = bf16[2560,640]{1,0:T(8,128)(2,1)} fusion(bf16[512,2560]{1,0:T(8,128)(2,1)} %gather_fusion, pred[512]{0:T(512)(128)(4,1)S(1)} %compare_and_fusion, bf16[512,640]{1,0:T(8,128)(2,1)S(1)} %copy-done.4, bf16[2560,640]{1,0:T(8,128)(2,1)} %param.7), kind=kOutput, calls=%fused_computation.1 | convolution fusion | flops 3367239680 | bytes 9830912 | tf_op jit(solution)/shard_map/dot_general | solution.py:26
  22.4 3.3 broadcast_select_fusion.2
  25.7 8.2 %collective-permute-start = (bf16[1280,640]{1,0:T(8,128)(2,1)}, bf16[1280,640]{1,0:T(8,128)(2,1)}, u32[]{:S(2)}, u32[]{:S(2)}) collective-permute-start(bf16[1280,640]{1,0:T(8,128)(2,1)} %broadcast_select_fusion.2), channel_id=1, source_target_pairs={{0,512},{16,528},{32,544},{48,560},{64,576},{80,592},{96,608},{112... | collective-permute-start | bytes 4915208 | tf_op jit(solution)/shard_map/ppermute | solution.py:14
  33.9 46.5 %collective-permute-done = bf16[1280,640]{1,0:T(8,128)(2,1)} collective-permute-done((bf16[1280,640]{1,0:T(8,128)(2,1)}, bf16[1280,640]{1,0:T(8,128)(2,1)}, u32[]{:S(2)}, u32[]{:S(2)}) %collective-permute-start) | collective-permute-done | bytes 1638432 | tf_op jit(solution)/shard_map/ppermute | solution.py:14
  80.4 5.5 multiply_reduce_fusion.2
  86.0 1.9 pad_maximum_fusion
  87.9 46.6 %psum.42 = f32[3]{0:T(128)S(1)} all-reduce(f32[3]{0:T(128)S(1)} %pad_maximum_fusion), channel_id=1, replica_groups=mesh['dp'=64,'tensor'=16] {'tensor'}, use_global_device_ids=true, to_apply=%region_3.4 | all-reduce | flops 3 | bytes 24 | tf_op jit(solution)/shard_map/psum | solution.py:52
  134.5 8.1 %collective-permute-start.1 = (f32[3]{0:T(128)S(1)}, f32[3]{0:T(128)S(1)}, u32[]{:S(2)}, u32[]{:S(2)}) collective-permute-start(f32[3]{0:T(128)S(1)} %psum.42), channel_id=1, source_target_pairs={{0,512},{16,528},{32,544},{48,560},{64,576},{80,592},{96,608},{112... | collective-permute-start | bytes 44 | tf_op jit(solution)/shard_map/ppermute | solution.py:14
  146.6 2.8 add_convert_fusion
  151.5 18.1 %collective-permute-start.2 = (bf16[640,640]{1,0:T(8,128)(2,1)}, bf16[640,640]{1,0:T(8,128)(2,1)S(1)}, u32[]{:S(2)}, u32[]{:S(2)}) collective-permute-start(bf16[640,640]{1,0:T(8,128)(2,1)} %broadcast_select_fusion.8), channel_id=1, source_target_pairs={{0,256},{16,272},{32,288},{48,304},{64,320},{80,336},{96,352},{112... | collective-permute-start | bytes 2457608 | tf_op jit(solution)/shard_map/ppermute | solution.py:14
  169.6 35.7 %collective-permute-done.2 = bf16[640,640]{1,0:T(8,128)(2,1)S(1)} collective-permute-done((bf16[640,640]{1,0:T(8,128)(2,1)}, bf16[640,640]{1,0:T(8,128)(2,1)S(1)}, u32[]{:S(2)}, u32[]{:S(2)}) %collective-permute-start.2) | collective-permute-done | bytes 819232 | tf_op jit(solution)/shard_map/ppermute | solution.py:14
  205.3 3.9 multiply_reduce_fusion.5
  209.2 2.0 pad_maximum_fusion.1
  211.2 20.1 %psum.43 = f32[3]{0:T(128)S(1)} all-reduce(f32[3]{0:T(128)S(1)} %pad_maximum_fusion.1), channel_id=1, replica_groups=mesh['dp'=64,'tensor'=16] {'tensor'}, use_global_device_ids=true, to_apply=%region_7.8 | all-reduce | flops 3 | bytes 24 | tf_op jit(solution)/shard_map/psum | solution.py:52
  231.3 1.9 collective-permute-start.3
  233.2 6.3 collective-permute-done.3
  239.5 1.9 collective-permute-start.4
  241.4 3.3 collective-permute-done.4
  250.3 1.9 collective-permute-start.5
  252.2 7.1 %collective-permute-done.5 = bf16[320,640]{1,0:T(8,128)(2,1)} collective-permute-done((bf16[320,640]{1,0:T(8,128)(2,1)}, bf16[320,640]{1,0:T(8,128)(2,1)}, u32[]{:S(2)}, u32[]{:S(2)}) %collective-permute-start.5) | collective-permute-done | bytes 409632 | tf_op jit(solution)/shard_map/ppermute | solution.py:14
  259.3 2.8 multiply_reduce_fusion.8
  262.1 2.0 pad_maximum_fusion.2
  264.1 21.4 %psum.44 = f32[3]{0:T(128)S(1)} all-reduce(f32[3]{0:T(128)S(1)} %pad_maximum_fusion.2), channel_id=1, replica_groups=mesh['dp'=64,'tensor'=16] {'tensor'}, use_global_device_ids=true, to_apply=%region_11.12 | all-reduce | flops 3 | bytes 24 | tf_op jit(solution)/shard_map/psum | solution.py:52
  285.6 3.8 collective-permute-start.6
  289.4 4.4 collective-permute-done.6
  293.8 1.9 collective-permute-start.7
  295.7 3.3 collective-permute-done.7
  299.0 1.9 collective-permute-start.8
  300.9 2.4 collective-permute-done.8
  307.9 4.8 collective-permute-start.9
  312.7 3.4 collective-permute-done.9
  317.0 2.1 pad_maximum_fusion.3
  319.0 21.2 %psum.45 = f32[3]{0:T(128)S(1)} all-reduce(f32[3]{0:T(128)S(1)} %pad_maximum_fusion.3), channel_id=1, replica_groups=mesh['dp'=64,'tensor'=16] {'tensor'}, use_global_device_ids=true, to_apply=%region_15.16 | all-reduce | flops 3 | bytes 24 | tf_op jit(solution)/shard_map/psum | solution.py:52
  340.2 3.6 collective-permute-start.10
  343.8 4.6 collective-permute-done.10
  350.3 3.3 collective-permute-done.11
  355.5 2.4 collective-permute-done.12
  357.9 4.2 collective-permute-start.13
  367.2 2.6 collective-permute-start.14
  369.9 2.7 collective-permute-done.14
  373.4 2.1 pad_maximum_fusion.4
  375.5 21.4 %psum.46 = f32[3]{0:T(128)S(1)} all-reduce(f32[3]{0:T(128)S(1)} %pad_maximum_fusion.4), channel_id=1, replica_groups=mesh['dp'=64,'tensor'=16] {'tensor'}, use_global_device_ids=true, to_apply=%region_19.20 | all-reduce | flops 3 | bytes 24 | tf_op jit(solution)/shard_map/psum | solution.py:52
  396.9 4.0 collective-permute-start.15
  401.0 4.2 collective-permute-done.15
  405.1 2.2 collective-permute-start.16
  407.4 3.0 collective-permute-done.16
  410.3 2.2 collective-permute-start.17
  412.6 2.1 collective-permute-done.17
  414.7 4.1 collective-permute-start.18
  420.5 2.9 collective-permute-start.19
  428.2 50.7 %collective-permute-start.20 = (bf16[40,640]{1,0:T(8,128)(2,1)S(1)}, bf16[40,640]{1,0:T(8,128)(2,1)S(1)}, u32[]{:S(2)}, u32[]{:S(2)}) collective-permute-start(bf16[40,640]{1,0:T(8,128)(2,1)S(1)} %broadcast_select_fusion.18), channel_id=1, source_target_pairs={{0,16},{16,0},{32,48},{48,32},{64,80},{80,64},{96,112},{112,96},{1... | collective-permute-start | bytes 153608 | tf_op jit(solution)/shard_map/ppermute | solution.py:14
  480.6 2.1 pad_maximum_fusion.5
  482.6 20.1 %psum.47 = f32[3]{0:T(128)S(1)} all-reduce(f32[3]{0:T(128)S(1)} %pad_maximum_fusion.5), channel_id=1, replica_groups=mesh['dp'=64,'tensor'=16] {'tensor'}, use_global_device_ids=true, to_apply=%region_23.24 | all-reduce | flops 3 | bytes 24 | tf_op jit(solution)/shard_map/psum | solution.py:52
  502.8 4.3 collective-permute-start.21
  507.0 3.9 collective-permute-done.21
  512.9 3.3 collective-permute-done.22
  516.2 1.9 collective-permute-start.23
  518.1 2.4 collective-permute-done.23
  520.5 4.6 collective-permute-start.24
  526.3 3.1 collective-permute-start.25
  530.6 14.9 %collective-permute-start.26 = (f32[3]{0:T(128)S(1)}, f32[3]{0:T(128)S(1)}, u32[]{:S(2)}, u32[]{:S(2)}) collective-permute-start(f32[3]{0:T(128)S(1)} %add.201), channel_id=1, source_target_pairs={{0,16},{16,0},{32,48},{48,32},{64,80},{80,64},{96,112},{112,96},{1... | collective-permute-start | bytes 44 | tf_op jit(solution)/shard_map/ppermute | solution.py:14
  550.9 86.3 %all-gather.2.cloned.1.call-done = bf16[2560,640]{1,0:T(8,128)(2,1)} async-done(((bf16[40,640]{1,0:T(8,128)(2,1)}), bf16[2560,640]{1,0:T(8,128)(2,1)}) %all-gather.2.cloned.1.call-update) | async-done | bytes 3276816 | tf_op jit(solution)/shard_map/all_gather | solution.py:71
  637.2 3.9 copy.8
  (66 shorter events, 31.3 us)
Async XLA Ops:
  7.2 1.8 copy-start
  7.2 630.0 %all-gather.2.cloned.1.call-start = ((), (), s32[]{:S(2)}) async-start(), calls=%async_computation | async-start | bytes 3328000 | tf_op jit(solution)/shard_map/all_gather | solution.py:71
  8.9 3.5 copy-start.4
  25.7 54.8 %collective-permute-start = (bf16[1280,640]{1,0:T(8,128)(2,1)}, bf16[1280,640]{1,0:T(8,128)(2,1)}, u32[]{:S(2)}, u32[]{:S(2)}) collective-permute-start(bf16[1280,640]{1,0:T(8,128)(2,1)} %broadcast_select_fusion.2), channel_id=1, source_target_pairs={{0,512},{16,528},{32,544},{48,560},{64,576},{80,592},{96,608},{112... | collective-permute-start | bytes 4915208 | tf_op jit(solution)/shard_map/ppermute | solution.py:14
  134.5 9.1 %collective-permute-start.1 = (f32[3]{0:T(128)S(1)}, f32[3]{0:T(128)S(1)}, u32[]{:S(2)}, u32[]{:S(2)}) collective-permute-start(f32[3]{0:T(128)S(1)} %psum.42), channel_id=1, source_target_pairs={{0,512},{16,528},{32,544},{48,560},{64,576},{80,592},{96,608},{112... | collective-permute-start | bytes 44 | tf_op jit(solution)/shard_map/ppermute | solution.py:14
  149.4 1.2 copy-start.1
  151.5 53.8 %collective-permute-start.2 = (bf16[640,640]{1,0:T(8,128)(2,1)}, bf16[640,640]{1,0:T(8,128)(2,1)S(1)}, u32[]{:S(2)}, u32[]{:S(2)}) collective-permute-start(bf16[640,640]{1,0:T(8,128)(2,1)} %broadcast_select_fusion.8), channel_id=1, source_target_pairs={{0,256},{16,272},{32,288},{48,304},{64,320},{80,336},{96,352},{112... | collective-permute-start | bytes 2457608 | tf_op jit(solution)/shard_map/ppermute | solution.py:14
  205.3 3.9 copy-start.2
  231.3 8.2 %collective-permute-start.3 = (f32[3]{0:T(128)S(1)}, f32[3]{0:T(128)S(1)}, u32[]{:S(2)}, u32[]{:S(2)}) collective-permute-start(f32[3]{0:T(128)S(1)} %psum.43), channel_id=1, source_target_pairs={{0,512},{16,528},{32,544},{48,560},{64,576},{80,592},{96,608},{112... | collective-permute-start | bytes 44 | tf_op jit(solution)/shard_map/ppermute | solution.py:14
  239.5 5.2 collective-permute-start.4
  250.3 9.0 %collective-permute-start.5 = (bf16[320,640]{1,0:T(8,128)(2,1)}, bf16[320,640]{1,0:T(8,128)(2,1)}, u32[]{:S(2)}, u32[]{:S(2)}) collective-permute-start(bf16[320,640]{1,0:T(8,128)(2,1)} %broadcast_select_fusion.12), channel_id=1, source_target_pairs={{0,128},{16,144},{32,160},{48,176},{64,192},{80,208},{96,224},{112... | collective-permute-start | bytes 1228808 | tf_op jit(solution)/shard_map/ppermute | solution.py:14
  285.6 8.2 %collective-permute-start.6 = (f32[3]{0:T(128)S(1)}, f32[3]{0:T(128)S(1)}, u32[]{:S(2)}, u32[]{:S(2)}) collective-permute-start(f32[3]{0:T(128)S(1)} %psum.44), channel_id=1, source_target_pairs={{0,512},{16,528},{32,544},{48,560},{64,576},{80,592},{96,608},{112... | collective-permute-start | bytes 44 | tf_op jit(solution)/shard_map/ppermute | solution.py:14
  293.8 5.2 collective-permute-start.7
  299.0 4.3 collective-permute-start.8
  307.9 241.4 %copy-start.3 = (f32[40,640]{1,0:T(8,128)S(1)}, f32[40,640]{1,0:T(8,128)}, u32[]{:S(2)}) copy-start(f32[40,640]{1,0:T(8,128)} %param.9) | copy-start | bytes 307204
  307.9 8.1 %collective-permute-start.9 = (bf16[160,640]{1,0:T(8,128)(2,1)S(1)}, bf16[160,640]{1,0:T(8,128)(2,1)S(1)}, u32[]{:S(2)}, u32[]{:S(2)}) collective-permute-start(bf16[160,640]{1,0:T(8,128)(2,1)S(1)} %broadcast_select_fusion.14), channel_id=1, source_target_pairs={{0,64},{16,80},{32,96},{48,112},{64,0},{80,16},{96,32},{112,48},{1... | collective-permute-start | bytes 614408 | tf_op jit(solution)/shard_map/ppermute | solution.py:14
  340.2 8.2 %collective-permute-start.10 = (f32[3]{0:T(128)S(1)}, f32[3]{0:T(128)S(1)}, u32[]{:S(2)}, u32[]{:S(2)}) collective-permute-start(f32[3]{0:T(128)S(1)} %psum.45), channel_id=1, source_target_pairs={{0,512},{16,528},{32,544},{48,560},{64,576},{80,592},{96,608},{112... | collective-permute-start | bytes 44 | tf_op jit(solution)/shard_map/ppermute | solution.py:14
  348.4 5.2 collective-permute-start.11
  353.6 4.3 collective-permute-start.12
  357.9 5.8 collective-permute-start.13
  367.2 5.4 collective-permute-start.14
  396.9 8.2 %collective-permute-start.15 = (f32[3]{0:T(128)S(1)}, f32[3]{0:T(128)S(1)}, u32[]{:S(2)}, u32[]{:S(2)}) collective-permute-start(f32[3]{0:T(128)S(1)} %psum.46), channel_id=1, source_target_pairs={{0,512},{16,528},{32,544},{48,560},{64,576},{80,592},{96,608},{112... | collective-permute-start | bytes 44 | tf_op jit(solution)/shard_map/ppermute | solution.py:14
  405.1 5.2 collective-permute-start.16
  410.3 4.3 collective-permute-start.17
  414.7 5.8 collective-permute-start.18
  420.5 4.3 collective-permute-start.19
  428.2 51.6 %collective-permute-start.20 = (bf16[40,640]{1,0:T(8,128)(2,1)S(1)}, bf16[40,640]{1,0:T(8,128)(2,1)S(1)}, u32[]{:S(2)}, u32[]{:S(2)}) collective-permute-start(bf16[40,640]{1,0:T(8,128)(2,1)S(1)} %broadcast_select_fusion.18), channel_id=1, source_target_pairs={{0,16},{16,0},{32,48},{48,32},{64,80},{80,64},{96,112},{112,96},{1... | collective-permute-start | bytes 153608 | tf_op jit(solution)/shard_map/ppermute | solution.py:14
  502.8 8.2 %collective-permute-start.21 = (f32[3]{0:T(128)S(1)}, f32[3]{0:T(128)S(1)}, u32[]{:S(2)}, u32[]{:S(2)}) collective-permute-start(f32[3]{0:T(128)S(1)} %psum.47), channel_id=1, source_target_pairs={{0,512},{16,528},{32,544},{48,560},{64,576},{80,592},{96,608},{112... | collective-permute-start | bytes 44 | tf_op jit(solution)/shard_map/ppermute | solution.py:14
  511.0 5.2 collective-permute-start.22
  516.2 4.3 collective-permute-start.23
  520.5 5.8 collective-permute-start.24
  526.3 4.3 collective-permute-start.25
  530.6 15.7 %collective-permute-start.26 = (f32[3]{0:T(128)S(1)}, f32[3]{0:T(128)S(1)}, u32[]{:S(2)}, u32[]{:S(2)}) collective-permute-start(f32[3]{0:T(128)S(1)} %add.201), channel_id=1, source_target_pairs={{0,16},{16,0},{32,48},{48,32},{64,80},{80,64},{96,112},{112,96},{1... | collective-permute-start | bytes 44 | tf_op jit(solution)/shard_map/ppermute | solution.py:14
Sparse Core Ops, SparseCore 0:
  551.0 86.1 all-gather.1
where the time goes:
time: 650 us; the launch traced here: 648 us
  waiting for transfers between devices  240 us (37%)
  starting transfers between devices  164 us (25%)
  blocking collectives  151 us (23%)
  other arithmetic  41.1 us (6%)
  between operations  29.6 us (5%)
  local copies, waits for them, and re-layouts  12.5 us (2%)
  matrix products  9.96 us (2%)
    ppermute x27, starting transfers between devices, from_partner(): return lax.ppermute(value, axis, pairs)  164 us
    ppermute x27, waiting for transfers between devices, from_partner(): return lax.ppermute(value, axis, pairs)  154 us
    psum x6, blocking collectives, body(): partials = lax.psum(partials, 'tensor')  151 us
    all_gather x1, waiting for transfers between devices, body(): new_weights = lax.all_gather(new_piece, 'dp', axis=0, tiled=True)  86.3 us
    reduce_sum x6, other arithmetic, body(): jnp.sum(first_vec * second_vec)  14.7 us
  transfers between devices with their start and end apart: 28, of which 28 were waited for; matrix products, arithmetic and copies ran while one was open for 0% of the time, Pallas kernels for 0%

commit v1 on v0

v1 whole, which is shorter than its diff:
```python
import jax
import jax.numpy as jnp
from jax import lax
from jax.experimental import pallas as pl
from jax.experimental.pallas import tpu as pltpu
from jax.sharding import PartitionSpec as P

epsilon = 1e-06
momentum_decay = 0.9
learning_rate = 0.25
LANES = 128


def gelu_tanh(values):
    return jax.nn.gelu(values, approximate=True)


def gram_kernel(slices_ref, table_ref, gram_ref):
    columns, replicas, rows = slices_ref.shape
    grads = jnp.dot(
        slices_ref[...].reshape(columns * replicas, rows),
        table_ref[...],
        preferred_element_type=jnp.float32,
    ).astype(jnp.bfloat16)
    total = jnp.zeros((replicas, replicas), jnp.float32)
    for column in range(columns):
        one = grads[column * replicas : (column + 1) * replicas]
        total += lax.dot_general(
            one, one, (((1,), (1,)), ((), ())), preferred_element_type=jnp.float32
        )
    total = jnp.concatenate([total] * (LANES // replicas), axis=1)

    @pl.when(pl.program_id(0) == 0)
    def _():
        gram_ref[...] = total

    @pl.when(pl.program_id(0) > 0)
    def _():
        gram_ref[...] += total


def gram(slices, table):
    columns, replicas, rows = slices.shape
    features = table.shape[1]
    block = 512
    return pl.pallas_call(
        gram_kernel,
        grid=(features // block,),
        in_specs=[
            pl.BlockSpec((columns, replicas, rows), lambda step: (0, 0, 0)),
            pl.BlockSpec((rows, block), lambda step: (0, step)),
        ],
        out_specs=pl.BlockSpec((replicas, LANES), lambda step: (0, 0)),
        out_shape=jax.ShapeDtypeStruct((replicas, LANES), jnp.float32),
        name="gram",
    )(slices, table)


def combine_kernel(gram_ref, slices_ref, sum_ref):
    columns, replicas, _ = slices_ref.shape
    inner = jnp.concatenate([gram_ref[...]] * (LANES // replicas), axis=0)
    row = lax.broadcasted_iota(jnp.int32, (LANES, LANES), 0)
    column = lax.broadcasted_iota(jnp.int32, (LANES, LANES), 1)
    weight = jnp.ones((LANES, 1), jnp.float32)
    for bit in reversed(range(replicas.bit_length() - 1)):
        stride = 2**bit
        own = jnp.where(row == column, inner, 0.0)
        cross = jnp.where((row + stride) % LANES == column, inner, 0.0)
        factors = []
        for axis in (1, 0):
            square = jnp.sum(own, axis=axis, keepdims=True)
            dot = jnp.sum(cross, axis=axis, keepdims=True)
            factors.append(1.0 - dot / (2.0 * (square + epsilon)))
        weight = weight * factors[0]
        scaled = factors[0] * inner * factors[1]
        scaled = scaled + pltpu.roll(scaled, stride, 0)
        inner = scaled + pltpu.roll(scaled, stride, 1)
    weight = weight[:replicas]
    for index in range(columns):
        sum_ref[pl.ds(index, 1), :] = jnp.sum(
            slices_ref[index].astype(jnp.float32) * weight, axis=0, keepdims=True
        )


def combine(gram_matrix, slices):
    columns, _, rows = slices.shape
    return pl.pallas_call(
        combine_kernel,
        out_shape=jax.ShapeDtypeStruct((columns, rows), jnp.float32),
        name="combine",
    )(gram_matrix, slices)


def exchange(value, axis):
    return lax.all_to_all(value, axis, 0, 0, tiled=True)


def share(value, axis):
    members = lax.axis_size(axis)
    return exchange(jnp.broadcast_to(value, (members, *value.shape)), axis)


def sum_everywhere(value):
    shards = lax.axis_size("tensor")
    height, width = value.shape
    part = exchange(value.reshape(shards, height // shards, width), "tensor")
    part = jnp.sum(part, axis=0)
    part = jnp.sum(share(part, "dp"), axis=0)
    return share(part, "tensor").reshape(height, width)


def update_kernel(
    features_ref, own_ref, total_ref, weights_ref, old_ref, momentum_ref, weights_out, momentum_out
):
    def product(features):
        return lax.dot_general(
            features, total_ref[...], (((1,), (1,)), ((), ())), preferred_element_type=jnp.float32
        )

    @pl.when(pl.program_id(0) == 0)
    def _():
        momentum_out[...] = momentum_decay * momentum_ref[...] + product(own_ref[...])

    step = momentum_decay * old_ref[...].astype(jnp.float32) + product(features_ref[...])
    weights_out[...] = (weights_ref[...].astype(jnp.float32) - learning_rate * step).astype(
        jnp.bfloat16
    )


def update(features, own_features, total, weights, old_momentum, momentum):
    height, hidden = weights.shape
    block = 512

    def blocked(array):
        return pl.BlockSpec((block, array.shape[1]), lambda step: (step, 0))

    def whole(array):
        return pl.BlockSpec(array.shape, lambda step: (0, 0))

    return pl.pallas_call(
        update_kernel,
        grid=(height // block,),
        in_specs=[
            blocked(features),
            whole(own_features),
            whole(total),
            blocked(weights),
            blocked(old_momentum),
            whole(momentum),
        ],
        out_specs=(blocked(weights), whole(momentum)),
        out_shape=(
            jax.ShapeDtypeStruct(weights.shape, jnp.bfloat16),
            jax.ShapeDtypeStruct(momentum.shape, jnp.float32),
        ),
        name="update",
    )(features, own_features, total, weights, old_momentum, momentum)


def body(token_ids, table, weights, targets, momentum):
    replicas = lax.axis_size("dp")
    replica_index = lax.axis_index("dp")
    owned_rows, hidden = momentum.shape
    rows = table.shape[0]
    columns = hidden // replicas
    old_momentum = lax.all_gather(momentum.astype(jnp.bfloat16), "dp", axis=0, tiled=True)

    chosen = token_ids[:, None] == lax.broadcasted_iota(jnp.int32, (token_ids.shape[0], rows), 1)
    counts = jnp.sum(chosen.astype(jnp.float32), axis=0, keepdims=True)
    wanted = lax.dot_general(
        targets,
        chosen.astype(jnp.bfloat16),
        (((0,), (0,)), ((), ())),
        preferred_element_type=jnp.float32,
    )
    preact = lax.dot_general(
        weights, table, (((0,), (1,)), ((), ())), preferred_element_type=jnp.float32
    )
    activated, pullback = jax.vjp(gelu_tanh, preact)
    row_grads = pullback(counts * activated - wanted)[0].astype(jnp.bfloat16)

    slices = exchange(row_grads.reshape(replicas, columns * rows // LANES, LANES), "dp")
    slices = slices.reshape(replicas, columns, rows).transpose(1, 0, 2)
    gram_matrix = sum_everywhere(gram(slices, table))
    total = combine(gram_matrix, slices).astype(jnp.bfloat16)
    total = share(total.reshape(columns * rows // LANES, LANES), "dp").reshape(hidden, rows)

    features = table.T
    own_features = lax.dynamic_slice_in_dim(features, replica_index * owned_rows, owned_rows, 0)
    return update(features, own_features, total, weights, old_momentum, momentum)


def solution(mesh):
    placed = (P("dp"), P(), P(None, "tensor"), P("dp", "tensor"), P("dp", "tensor"))
    return jax.shard_map(
        body,
        mesh=mesh,
        in_specs=placed,
        out_specs=(P(None, "tensor"), P("dp", "tensor")),
        check_vma=False,
    )
```

time: 650 us -> 171 us (0.26)
  waiting for transfers between devices: 240 us -> 16.7 us
  starting transfers between devices: 164 us -> 6.36 us
  blocking collectives: 151 us -> 96 us
  other arithmetic: 41.1 us -> 3.31 us
  Pallas kernels: 0 us -> 18.7 us
  between operations: 29.6 us -> 14.1 us
    ppermute x27 -> x0, starting transfers between devices: 164 us -> none  [from_partner(): return lax.ppermute(value, axis, pairs)]
    ppermute x27 -> x0, waiting for transfers between devices: 154 us -> none  [from_partner(): return lax.ppermute(value, axis, pairs)]
    psum x6 -> x0, blocking collectives: 151 us -> none  [body(): partials = lax.psum(partials, 'tensor')]
    all_to_all x0 -> x4, blocking collectives: none -> 96 us  [exchange(): return lax.all_to_all(value, axis, 0, 0, tiled=True)]
    all_gather x1, waiting for transfers between devices: 86.3 us -> 0.01 us  [body(): lax.all_gather(momentum.astype(jnp.bfloat16), 'dp', axis=0, tiled=True)]
    pallas_call x0 -> x3, Pallas kernels: none -> 18.7 us  [the longest x1 8.77 us: update(): pl.pallas_call(update_kernel, grid=(height // block,), in_specs=[blocked(...]
    all_to_all x0 -> x1, waiting for transfers between devices: none -> 16.7 us  [exchange(): return lax.all_to_all(value, axis, 0, 0, tiled=True)]
    reduce_sum x6 -> x3, other arithmetic: 14.7 us -> 0.97 us  [the longest x1 0.86 us: body(): counts = jnp.sum(chosen.astype(jnp.float32), axis=0, keepdims=True)]
  transfers between devices with their start and end apart: 28 -> 2, of which waited for: 28 -> 1; matrix products, arithmetic and copies ran while one was open for 0% -> 10% of each run, Pallas kernels for 0% -> 6%
where the time goes in v1:
time: 171 us; the launch traced here: 170 us
  blocking collectives  96 us (56%)
  Pallas kernels  18.7 us (11%)
  waiting for transfers between devices  16.7 us (10%)
  between operations  14.1 us (8%)
  local copies, waits for them, and re-layouts  8.87 us (5%)
  starting transfers between devices  6.36 us (4%)
  matrix products  6.14 us (4%)
  other arithmetic  3.31 us (2%)
    all_to_all x4, blocking collectives, exchange(): return lax.all_to_all(value, axis, 0, 0, tiled=True)  96 us
    all_to_all x1, waiting for transfers between devices, exchange(): return lax.all_to_all(value, axis, 0, 0, tiled=True)  16.7 us
    pallas_call x1, Pallas kernels, update(): pl.pallas_call(update_kernel, grid=(height // block,), in_specs=[blocked(...  8.77 us
    pallas_call x1, Pallas kernels, gram(): pl.pallas_call(gram_kernel, grid=(features // block,), in_specs=[pl.Block...  7.15 us
    all_to_all x1, starting transfers between devices, exchange(): return lax.all_to_all(value, axis, 0, 0, tiled=True)  6.33 us
    dot_general x1, matrix products, body(): lax.dot_general(weights, table, (((0,), (1,)), ((), ())), preferred_eleme...  4.64 us
  transfers between devices with their start and end apart: 2, of which 1 were waited for; matrix products, arithmetic and copies ran while one was open for 10% of the time, Pallas kernels for 6%

profile of v1, /device:TPU:1, one launch (start us, length us, event | category | flops | bytes accessed | tf_op | source)
XLA Modules:
  0.0 170.3 jit_solution(12953999149271849084)
XLA Ops:
  7.2 0.0 copy-start
  7.2 0.0 all-gather.2.cloned.1.call-start
  7.2 1.6 convert_element_type.16
  8.8 0.0 all-gather.2.cloned.1.call-update
  8.8 0.9 convert_reduce_fusion
  9.7 0.0 copy-start.2
  9.7 4.6 %fusion.9 = f32[640,512]{1,0:T(8,128)S(1)} fusion(bf16[2560,640]{1,0:T(8,128)(2,1)} %weights_ref.1, bf16[512,2560]{1,0:T(8,128)(2,1)} %table_ref.1), kind=kOutput, calls=%fused_computation.16 | convolution fusion | flops 1677721600 | bytes 7208960 | tf_op jit(solution)/shard_map/dot_general | solution.py:176
  14.4 0.0 copy-done
  14.4 0.0 copy-done.2
  14.4 1.5 fusion.7
  15.9 0.4 reshape.24
  16.3 38.5 %all_to_all.25 = bf16[64,40,128]{2,1,0:T(8,128)(2,1)S(1)} all-to-all(bf16[64,40,128]{2,1,0:T(8,128)(2,1)S(1)} %reshape.24), channel_id=1, replica_groups=mesh['dp'=64,'tensor'=16] {'dp'}, dimensions={0} | all-to-all | bytes 1310720 | tf_op jit(solution)/shard_map/all_to_all | solution.py:95
  54.8 0.4 reshape.25
  55.2 1.2 copy.26
  56.4 7.2 %gram.1 = f32[64,128]{1,0:T(8,128)} custom-call(bf16[10,64,512]{2,1,0:T(8,128)(2,1)} %bitcast.18, bf16[512,2560]{1,0:T(8,128)(2,1)} %table_ref.1), custom_call_target="tpu_custom_call" | custom-call | tf_op jit(solution)/shard_map/gram/pallas_call | solution.py:46
  63.6 24.1 %all_to_all.26 = f32[16,4,128]{2,1,0:T(4,128)S(1)} all-to-all(f32[16,4,128]{2,1,0:T(4,128)} %bitcast.20), channel_id=1, replica_groups=mesh['dp'=64,'tensor'=16] {'tensor'}, dimensions={0} | all-to-all | bytes 65536 | tf_op jit(solution)/shard_map/all_to_all | solution.py:95
  87.7 18.8 %all_to_all.27 = f32[64,4,128]{2,1,0:T(4,128)S(1)} all-to-all(f32[64,4,128]{2,1,0:T(4,128)S(1)} %broadcast_in_dim.11), channel_id=1, replica_groups=mesh['dp'=64,'tensor'=16] {'dp'}, dimensions={0} | all-to-all | bytes 262144 | tf_op jit(solution)/shard_map/all_to_all | solution.py:95
  106.5 0.1 reduce_sum.29
  106.6 14.6 %all_to_all.28 = f32[16,4,128]{2,1,0:T(4,128)} all-to-all(f32[16,4,128]{2,1,0:T(4,128)S(1)} %broadcast_in_dim.12), channel_id=1, replica_groups=mesh['dp'=64,'tensor'=16] {'tensor'}, dimensions={0} | all-to-all | bytes 65536 | tf_op jit(solution)/shard_map/all_to_all | solution.py:95
  121.2 2.8 %combine.1 = f32[10,512]{1,0:T(8,128)} custom-call(f32[64,128]{1,0:T(8,128)} %bitcast.21, bf16[10,64,512]{2,1,0:T(8,128)(2,1)} %bitcast.19), custom_call_target="tpu_custom_call" | custom-call | tf_op jit(solution)/shard_map/combine/pallas_call | solution.py:87
  124.0 0.8 convert_element_type.15
  124.8 0.9 broadcast_in_dim.13
  125.7 6.3 %all-to-all-start.4 = ((bf16[64,40,128]{2,1,0:T(8,128)(2,1)}), bf16[64,40,128]{2,1,0:T(8,128)(2,1)}, u32[]{:S(2)}, u32[]{:S(2)}) async-start(bf16[64,40,128]{2,1,0:T(8,128)(2,1)} %broadcast_in_dim.13), calls=%async_computation.4 | async-start | bytes 1310720 | tf_op jit(solution)/shard_map/all_to_all | solution.py:95
  132.0 3.0 %copy.18 = bf16[512,2560]{0,1:T(8,128)(2,1)S(1)} copy(bf16[512,2560]{1,0:T(8,128)(2,1)} %table_ref.1) | data formatting | bytes 5242880 | tf_op args[1]
  135.0 0.0 copy-start.1
  135.1 0.7 dynamic-slice_bitcast_fusion.own_ref
  135.7 16.7 %all-to-all-done.4 = bf16[64,40,128]{2,1,0:T(8,128)(2,1)} async-done(((bf16[64,40,128]{2,1,0:T(8,128)(2,1)}), bf16[64,40,128]{2,1,0:T(8,128)(2,1)}, u32[]{:S(2)}, u32[]{:S(2)}) %all-to-all-start.4) | async-done | bytes 655392 | tf_op jit(solution)/shard_map/all_to_all | solution.py:95
  152.5 2.2 %reshape.29.total_ref = bf16[640,512]{1,0:T(8,128)(2,1)} reshape(bf16[64,40,128]{2,1,0:T(8,128)(2,1)} %all-to-all-done.4) | data formatting | bytes 1310720 | tf_op jit(solution)/shard_map/reshape | solution.py:186
  154.7 0.0 all-gather.2.cloned.1.call-done.old_ref
  154.7 0.0 copy-done.1
  154.7 8.8 %update.1 = (bf16[2560,640]{1,0:T(8,128)(2,1)}, f32[40,640]{1,0:T(8,128)}) custom-call(bf16[2560,512]{1,0:T(8,128)(2,1)} %bitcast.17, bf16[40,512]{1,0:T(8,128)(2,1)} %dynamic-slice_bitcast_fusion.own_ref, bf16[640,512]{1,0:T(8,128)(2,1)} %reshape.29.total_ref, bf16[2560,640]{1,0:T(8,128)(2,1)} %weights_ref.1, ...), custom_call_target="tpu_custom_call" | custom-call | tf_op jit(solution)/shard_map/update/pallas_call | solution.py:140
  (4 shorter events, 0.1 us)
Async XLA Ops:
  7.2 7.2 %copy-start = (bf16[512,640]{1,0:T(8,128)(2,1)S(1)}, bf16[512,640]{1,0:T(8,128)(2,1)}, u32[]{:S(2)}) copy-start(bf16[512,640]{1,0:T(8,128)(2,1)} %param.8) | copy-start | bytes 1966084
  7.2 147.5 %all-gather.2.cloned.1.call-start = ((), (), s32[]{:S(2)}) async-start(), calls=%async_computation.5 | async-start | bytes 3328000 | tf_op jit(solution)/shard_map/all_gather | solution.py:166
  9.7 4.7 %copy-start.2 = (s32[512]{0:T(512)S(1)}, s32[512]{0:T(512)}, u32[]{:S(2)}) copy-start(s32[512]{0:T(512)} %param.5) | copy-start | bytes 6148
  125.7 26.8 %all-to-all-start.4 = ((bf16[64,40,128]{2,1,0:T(8,128)(2,1)}), bf16[64,40,128]{2,1,0:T(8,128)(2,1)}, u32[]{:S(2)}, u32[]{:S(2)}) async-start(bf16[64,40,128]{2,1,0:T(8,128)(2,1)} %broadcast_in_dim.13), calls=%async_computation.4 | async-start | bytes 1310720 | tf_op jit(solution)/shard_map/all_to_all | solution.py:95
  135.0 19.6 %copy-start.1 = (bf16[512,2560]{0,1:T(8,128)(2,1)}, bf16[512,2560]{0,1:T(8,128)(2,1)S(1)}, u32[]{:S(2)}) copy-start(bf16[512,2560]{0,1:T(8,128)(2,1)S(1)} %copy.18) | copy-start | bytes 7864324
Sparse Core Ops, SparseCore 0:
  13.0 104.3 all-gather.1

commit v2 on v1

v2 whole, which is shorter than its diff:
```python
import jax
import jax.numpy as jnp
from jax import lax
from jax.experimental import pallas as pl
from jax.experimental.pallas import tpu as pltpu
from jax.sharding import PartitionSpec as P

epsilon = 1e-06
momentum_decay = 0.9
learning_rate = 0.25
LANES = 128
WIDE = 256


def gelu_tanh(values):
    return jax.nn.gelu(values, approximate=True)


def gram_kernel(slices_ref, table_ref, gram_ref, total_ref):
    columns, replicas, rows = slices_ref.shape
    step = pl.program_id(0)
    grads = jnp.dot(
        slices_ref[...].reshape(columns * replicas, rows),
        table_ref[...],
        preferred_element_type=jnp.float32,
    ).astype(jnp.bfloat16)
    for start in range(0, columns * replicas, WIDE):
        some = grads[start : start + WIDE]
        height = some.shape[0]
        product = lax.dot_general(
            some, some, (((1,), (1,)), ((), ())), preferred_element_type=jnp.float32
        )
        if start == 0:
            total_ref[...] = jnp.where(step == 0, 0.0, total_ref[...]) + product
        else:
            total_ref[:height, :height] += product

    @pl.when(step == pl.num_programs(0) - 1)
    def _():
        total = jnp.zeros((replicas, replicas), jnp.float32)
        for start in range(0, WIDE, replicas):
            total += total_ref[start : start + replicas, start : start + replicas]
        gram_ref[...] = jnp.concatenate([total] * (LANES // replicas), axis=1)


def gram(slices, table):
    columns, replicas, rows = slices.shape
    features = table.shape[1]
    block = 512
    return pl.pallas_call(
        gram_kernel,
        grid=(features // block,),
        in_specs=[
            pl.BlockSpec((columns, replicas, rows), lambda step: (0, 0, 0)),
            pl.BlockSpec((rows, block), lambda step: (0, step)),
        ],
        out_specs=pl.BlockSpec((replicas, LANES), lambda step: (0, 0)),
        out_shape=jax.ShapeDtypeStruct((replicas, LANES), jnp.float32),
        scratch_shapes=[pltpu.VMEM((WIDE, WIDE), jnp.float32)],
        name="gram",
    )(slices, table)


def combine_kernel(gram_ref, slices_ref, sum_ref, flat_ref):
    columns, replicas, rows = slices_ref.shape
    inner = jnp.concatenate([gram_ref[...]] * (LANES // replicas), axis=0)
    row = lax.broadcasted_iota(jnp.int32, (LANES, LANES), 0)
    column = lax.broadcasted_iota(jnp.int32, (LANES, LANES), 1)
    weight = jnp.ones((LANES, 1), jnp.float32)
    for bit in reversed(range(replicas.bit_length() - 1)):
        stride = 2**bit
        own = jnp.where(row == column, inner, 0.0)
        cross = jnp.where((row + stride) % LANES == column, inner, 0.0)
        factors = []
        for axis in (1, 0):
            square = jnp.sum(own, axis=axis, keepdims=True)
            dot = jnp.sum(cross, axis=axis, keepdims=True)
            factors.append(1.0 - dot / (2.0 * (square + epsilon)))
        weight = weight * factors[0]
        scaled = factors[0] * inner * factors[1]
        scaled = scaled + pltpu.roll(scaled, stride, 0)
        inner = scaled + pltpu.roll(scaled, stride, 1)
    weight = weight[:replicas]
    for index in range(columns):
        total = jnp.sum(slices_ref[index].astype(jnp.float32) * weight, axis=0, keepdims=True)
        for part in range(rows // LANES):
            flat_ref[pl.ds(index * rows // LANES + part, 1), :] = total[
                :, part * LANES : (part + 1) * LANES
            ]
    flat = flat_ref[...].astype(jnp.bfloat16)
    for replica in range(replicas):
        sum_ref[replica] = flat


def combine(gram_matrix, slices):
    columns, replicas, rows = slices.shape
    height = columns * rows // LANES
    return pl.pallas_call(
        combine_kernel,
        out_shape=jax.ShapeDtypeStruct((replicas, height, LANES), jnp.bfloat16),
        scratch_shapes=[pltpu.VMEM((height, LANES), jnp.float32)],
        name="combine",
    )(gram_matrix, slices)


def exchange(value, axis):
    return lax.all_to_all(value, axis, 0, 0, tiled=True)


def share(value, axis):
    members = lax.axis_size(axis)
    return exchange(jnp.broadcast_to(value, (members, *value.shape)), axis)


def sum_everywhere(value):
    shards = lax.axis_size("tensor")
    height, width = value.shape
    part = exchange(value.reshape(shards, height // shards, width), "tensor")
    part = jnp.sum(part, axis=0)
    part = jnp.sum(share(part, "dp"), axis=0)
    return share(part, "tensor").reshape(height, width)


def update_kernel(
    first_row_ref,
    total_ref,
    features_ref,
    weights_ref,
    old_ref,
    momentum_ref,
    weights_out,
    momentum_out,
    flat_ref,
    rows_ref,
    adasum_ref,
):
    block, owned_rows = weights_out.shape[0], momentum_ref.shape[0]
    step = pl.program_id(0)
    first_row = first_row_ref[0]

    @pl.when(step == 0)
    def _():
        flat_ref[...] = total_ref[...].astype(jnp.float32).reshape(flat_ref.shape)
        height, width = rows_ref.shape
        parts = width // LANES
        for part in range(parts):
            rows_ref[:, part * LANES : (part + 1) * LANES] = flat_ref[
                pl.ds(part, height, stride=parts), :
            ].astype(jnp.bfloat16)

    adasum = lax.dot_general(
        features_ref[...],
        rows_ref[...],
        (((1,), (1,)), ((), ())),
        preferred_element_type=jnp.float32,
    )
    new_momentum = momentum_decay * old_ref[...].astype(jnp.float32) + adasum
    weights_out[...] = (
        weights_ref[...].astype(jnp.float32) - learning_rate * new_momentum
    ).astype(jnp.bfloat16)

    @pl.when(step == first_row // block)
    def _():
        adasum_ref[...] = adasum
        own = pl.ds(pl.multiple_of(first_row % block, 8), owned_rows)
        momentum_out[...] = momentum_decay * momentum_ref[...] + adasum_ref[own, :]


def update(first_row, total, features, weights, old_momentum, momentum):
    height, hidden = weights.shape
    rows = features.shape[1]
    block = 320
    blocked = pl.BlockSpec((block, hidden), lambda step, _: (step, 0))
    return pl.pallas_call(
        update_kernel,
        grid_spec=pltpu.PrefetchScalarGridSpec(
            num_scalar_prefetch=1,
            grid=(height // block,),
            in_specs=[
                pl.BlockSpec(total.shape, lambda step, _: (0, 0, 0)),
                pl.BlockSpec((block, rows), lambda step, _: (step, 0)),
                blocked,
                blocked,
                pl.BlockSpec(momentum.shape, lambda step, _: (0, 0)),
            ],
            out_specs=(blocked, pl.BlockSpec(momentum.shape, lambda step, _: (0, 0))),
            scratch_shapes=[
                pltpu.VMEM((hidden * rows // LANES, LANES), jnp.float32),
                pltpu.VMEM((hidden, rows), jnp.bfloat16),
                pltpu.VMEM((block, hidden), jnp.float32),
            ],
        ),
        out_shape=(
            jax.ShapeDtypeStruct(weights.shape, jnp.bfloat16),
            jax.ShapeDtypeStruct(momentum.shape, jnp.float32),
        ),
        name="update",
    )(
        first_row.reshape(1),
        total,
        features,
        weights,
        old_momentum,
        momentum,
    )


def body(token_ids, table, weights, targets, momentum):
    replicas = lax.axis_size("dp")
    replica_index = lax.axis_index("dp")
    owned_rows, hidden = momentum.shape
    rows = table.shape[0]
    columns = hidden // replicas
    old_momentum = lax.all_gather(momentum.astype(jnp.bfloat16), "dp", axis=0, tiled=True)

    chosen = token_ids[:, None] == lax.broadcasted_iota(jnp.int32, (token_ids.shape[0], rows), 1)
    counts = jnp.sum(chosen.astype(jnp.float32), axis=0, keepdims=True)
    wanted = lax.dot_general(
        targets,
        chosen.astype(jnp.bfloat16),
        (((0,), (0,)), ((), ())),
        preferred_element_type=jnp.float32,
    )
    preact = lax.dot_general(
        weights, table, (((0,), (1,)), ((), ())), preferred_element_type=jnp.float32
    )
    activated, pullback = jax.vjp(gelu_tanh, preact)
    row_grads = pullback(counts * activated - wanted)[0].astype(jnp.bfloat16)

    slices = exchange(row_grads.reshape(replicas, columns * rows // LANES, LANES), "dp")
    slices = slices.reshape(replicas, columns, rows).transpose(1, 0, 2)
    gram_matrix = sum_everywhere(gram(slices, table))
    total = exchange(combine(gram_matrix, slices), "dp")
    first_row = replica_index * owned_rows
    return update(first_row, total, table.T, weights, old_momentum, momentum)


def solution(mesh):
    placed = (P("dp"), P(), P(None, "tensor"), P("dp", "tensor"), P("dp", "tensor"))
    return jax.shard_map(
        body,
        mesh=mesh,
        in_specs=placed,
        out_specs=(P(None, "tensor"), P("dp", "tensor")),
        check_vma=False,
    )
```

time: 171 us -> 167 us (0.977)
  local copies, waits for them, and re-layouts: 8.87 us -> 4.67 us
    reshape x2 -> x0, local copies, waits for them, and re-layouts: 2.23 us -> none  [the longest x1 2.21 us: body(): share(total.reshape(columns * rows // LANES, LANES), 'dp')]
  transfers between devices with their start and end apart: 2 -> 2, of which waited for: 1 -> 1; matrix products, arithmetic and copies ran while one was open for 10% -> 7% of each run, Pallas kernels for 6% -> 6%
where the time goes in v2:
time: 167 us
  blocking collectives  95.9 us (57%)
  Pallas kernels  19.4 us (12%)
  waiting for transfers between devices  17.8 us (11%)
  between operations  14.1 us (8%)
  starting transfers between devices  6.36 us (4%)
  matrix products  6.14 us (4%)
  local copies, waits for them, and re-layouts  4.67 us (3%)
  other arithmetic  2.55 us (2%)
    all_to_all x4, blocking collectives, exchange(): return lax.all_to_all(value, axis, 0, 0, tiled=True)  95.9 us
    all_to_all x1, waiting for transfers between devices, exchange(): return lax.all_to_all(value, axis, 0, 0, tiled=True)  17.8 us
    pallas_call x1, Pallas kernels, update(): pl.pallas_call(update_kernel, grid_spec=pltpu.PrefetchScalarGridSpec(num_...  9.52 us
    pallas_call x1, Pallas kernels, gram(): pl.pallas_call(gram_kernel, grid=(features // block,), in_specs=[pl.Block...  6.61 us
    all_to_all x1, starting transfers between devices, exchange(): return lax.all_to_all(value, axis, 0, 0, tiled=True)  6.33 us
    dot_general x1, matrix products, body(): lax.dot_general(weights, table, (((0,), (1,)), ((), ())), preferred_eleme...  4.64 us
  transfers between devices with their start and end apart: 2, of which 1 were waited for; matrix products, arithmetic and copies ran while one was open for 7% of the time, Pallas kernels for 6%

profile of v2, /device:TPU:1, one launch (start us, length us, event | category | flops | bytes accessed | tf_op | source)
XLA Modules:
  0.0 166.8 jit_solution(9932283797376956818)
XLA Ops:
  7.2 0.0 copy-start
  7.2 0.0 all-gather.2.cloned.1.call-start
  7.2 1.6 convert_element_type.12
  8.8 0.0 all-gather.2.cloned.1.call-update
  8.8 0.9 convert_reduce_fusion
  9.7 0.0 copy-start.2
  9.7 4.6 %fusion.9 = f32[640,512]{1,0:T(8,128)S(1)} fusion(bf16[2560,640]{1,0:T(8,128)(2,1)} %weights_ref.1, bf16[512,2560]{1,0:T(8,128)(2,1)} %table_ref.1), kind=kOutput, calls=%fused_computation.15 | convolution fusion | flops 1677721600 | bytes 7208960 | tf_op jit(solution)/shard_map/dot_general | solution.py:224
  14.4 0.0 copy-done
  14.4 0.0 copy-done.2
  14.4 1.5 fusion.7
  15.9 0.4 reshape.22
  16.3 38.5 %all_to_all.25 = bf16[64,40,128]{2,1,0:T(8,128)(2,1)S(1)} all-to-all(bf16[64,40,128]{2,1,0:T(8,128)(2,1)S(1)} %reshape.22), channel_id=1, replica_groups=mesh['dp'=64,'tensor'=16] {'dp'}, dimensions={0} | all-to-all | bytes 1310720 | tf_op jit(solution)/shard_map/all_to_all | solution.py:107
  54.8 0.4 reshape.23
  55.2 1.2 copy.22
  56.4 6.6 %gram.1 = f32[64,128]{1,0:T(8,128)} custom-call(bf16[10,64,512]{2,1,0:T(8,128)(2,1)} %bitcast.17, bf16[512,2560]{1,0:T(8,128)(2,1)} %table_ref.1), custom_call_target="tpu_custom_call" | custom-call | tf_op jit(solution)/shard_map/gram/pallas_call | solution.py:50
  63.0 24.1 %all_to_all.26 = f32[16,4,128]{2,1,0:T(4,128)S(1)} all-to-all(f32[16,4,128]{2,1,0:T(4,128)} %bitcast.19), channel_id=1, replica_groups=mesh['dp'=64,'tensor'=16] {'tensor'}, dimensions={0} | all-to-all | bytes 65536 | tf_op jit(solution)/shard_map/all_to_all | solution.py:107
  87.2 18.6 %all_to_all.27 = f32[64,4,128]{2,1,0:T(4,128)S(1)} all-to-all(f32[64,4,128]{2,1,0:T(4,128)S(1)} %broadcast_in_dim.8), channel_id=1, replica_groups=mesh['dp'=64,'tensor'=16] {'dp'}, dimensions={0} | all-to-all | bytes 262144 | tf_op jit(solution)/shard_map/all_to_all | solution.py:107
  105.8 0.1 reduce_sum.29
  105.9 14.6 %all_to_all.28 = f32[16,4,128]{2,1,0:T(4,128)} all-to-all(f32[16,4,128]{2,1,0:T(4,128)S(1)} %broadcast_in_dim.9), channel_id=1, replica_groups=mesh['dp'=64,'tensor'=16] {'tensor'}, dimensions={0} | all-to-all | bytes 65536 | tf_op jit(solution)/shard_map/all_to_all | solution.py:107
  120.5 0.0 copy-start.1
  120.5 3.2 %combine.1 = bf16[64,40,128]{2,1,0:T(8,128)(2,1)} custom-call(f32[64,128]{1,0:T(8,128)} %bitcast.20, bf16[10,64,512]{2,1,0:T(8,128)(2,1)} %bitcast.18), custom_call_target="tpu_custom_call" | custom-call | tf_op jit(solution)/shard_map/combine/pallas_call | solution.py:98
  123.7 6.3 %all-to-all-start.4 = ((bf16[64,40,128]{2,1,0:T(8,128)(2,1)}), bf16[64,40,128]{2,1,0:T(8,128)(2,1)}, u32[]{:S(2)}, u32[]{:S(2)}) async-start(bf16[64,40,128]{2,1,0:T(8,128)(2,1)} %combine.1), calls=%async_computation.4 | async-start | bytes 1310720 | tf_op jit(solution)/shard_map/all_to_all | solution.py:107
  130.0 0.0 copy-done.1
  130.0 2.6 %copy.18 = bf16[512,2560]{0,1:T(8,128)(2,1)} copy(bf16[512,2560]{1,0:T(8,128)(2,1)S(1)} %copy-done.1) | data formatting | bytes 5242880 | tf_op args[1]
  132.7 17.8 %all-to-all-done.4.total_ref = bf16[64,40,128]{2,1,0:T(8,128)(2,1)} async-done(((bf16[64,40,128]{2,1,0:T(8,128)(2,1)}), bf16[64,40,128]{2,1,0:T(8,128)(2,1)}, u32[]{:S(2)}, u32[]{:S(2)}) %all-to-all-start.4) | async-done | bytes 655392 | tf_op jit(solution)/shard_map/all_to_all | solution.py:107
  150.5 0.0 all-gather.2.cloned.1.call-done.old_ref
  150.5 9.5 %update.1 = (bf16[2560,640]{1,0:T(8,128)(2,1)}, f32[40,640]{1,0:T(8,128)}) custom-call(s32[1]{0:T(128)} %bitcast.first_row_ref, bf16[64,40,128]{2,1,0:T(8,128)(2,1)} %all-to-all-done.4.total_ref, bf16[2560,512]{1,0:T(8,128)(2,1)} %bitcast.16, bf16[2560,640]{1,0:T(8,128)(2,1)} %weights_ref.1, bf16[2560,640]{1,0:T(8,128)(2,1)} %all-gather.2.cloned.1.call-done.old_ref, ...), custom_call_target="tpu_custom_call" | custom-call | tf_op jit(solution)/shard_map/update/pallas_call | solution.py:174
  (3 shorter events, 0.1 us)
Async XLA Ops:
  7.2 7.2 %copy-start = (bf16[512,640]{1,0:T(8,128)(2,1)S(1)}, bf16[512,640]{1,0:T(8,128)(2,1)}, u32[]{:S(2)}) copy-start(bf16[512,640]{1,0:T(8,128)(2,1)} %param.8) | copy-start | bytes 1966084
  7.2 143.3 %all-gather.2.cloned.1.call-start = ((), (), s32[]{:S(2)}) async-start(), calls=%async_computation.5 | async-start | bytes 3328000 | tf_op jit(solution)/shard_map/all_gather | solution.py:214
  9.7 4.7 %copy-start.2 = (s32[512]{0:T(512)S(1)}, s32[512]{0:T(512)}, u32[]{:S(2)}) copy-start(s32[512]{0:T(512)} %param.5) | copy-start | bytes 6148
  120.5 9.6 %copy-start.1 = (bf16[512,2560]{1,0:T(8,128)(2,1)S(1)}, bf16[512,2560]{1,0:T(8,128)(2,1)}, u32[]{:S(2)}) copy-start(bf16[512,2560]{1,0:T(8,128)(2,1)} %table_ref.1) | copy-start | bytes 7864324
  123.7 26.8 %all-to-all-start.4 = ((bf16[64,40,128]{2,1,0:T(8,128)(2,1)}), bf16[64,40,128]{2,1,0:T(8,128)(2,1)}, u32[]{:S(2)}, u32[]{:S(2)}) async-start(bf16[64,40,128]{2,1,0:T(8,128)(2,1)} %combine.1), calls=%async_computation.4 | async-start | bytes 1310720 | tf_op jit(solution)/shard_map/all_to_all | solution.py:107
Sparse Core Ops, SparseCore 0:
  13.0 103.9 all-gather.1

commit v3 on v2

v3 whole, which is shorter than its diff:
```python
import jax
import jax.numpy as jnp
from jax import lax
from jax.experimental import pallas as pl
from jax.experimental.pallas import tpu as pltpu
from jax.sharding import Mesh
from jax.sharding import PartitionSpec as P

epsilon = 1e-06
momentum_decay = 0.9
learning_rate = 0.25
LANES = 128
WIDE = 256
FACTORS = (8, 4, 2)
CHIPS = ("y", "x")
REPLICAS = ("y", "x", "core")
CORES_FIRST = ("core", "y", "x")


def gelu_tanh(values):
    return jax.nn.gelu(values, approximate=True)


def gram_kernel(slices_ref, kernel_ref, gram_ref):
    columns, replicas, rows = slices_ref.shape
    values = slices_ref[...].reshape(columns * replicas, rows)
    high = kernel_ref[...].astype(jnp.bfloat16)
    low = (kernel_ref[...] - high.astype(jnp.float32)).astype(jnp.bfloat16)
    images = (
        jnp.dot(values, high, preferred_element_type=jnp.float32)
        + jnp.dot(values, low, preferred_element_type=jnp.float32)
    ).astype(jnp.bfloat16)
    total = jnp.zeros((replicas, replicas), jnp.float32)
    for start in range(0, columns * replicas, WIDE):
        products = lax.dot_general(
            values[start : start + WIDE],
            images[start : start + WIDE],
            (((1,), (1,)), ((), ())),
            preferred_element_type=jnp.float32,
        )
        for own in range(0, products.shape[0], replicas):
            total += products[own : own + replicas, own : own + replicas]
    height = replicas // 4
    for half in range(2):
        first = 2 * half * height
        gram_ref[half] = jnp.concatenate(
            [total[first : first + height], total[first + height : first + 2 * height]], axis=1
        )


def gram(slices, kernel):
    replicas = slices.shape[1]
    return pl.pallas_call(
        gram_kernel,
        out_shape=jax.ShapeDtypeStruct((2, replicas // 4, 2 * replicas), jnp.float32),
        name="gram",
    )(slices, kernel)


def combine_kernel(gram_ref, slices_ref, sum_ref, flat_ref):
    columns, replicas, rows = slices_ref.shape
    full = []
    for half in range(2):
        for side in range(2):
            lines = gram_ref[half, :, side * replicas : (side + 1) * replicas]
            full.append(jnp.concatenate([lines] * (LANES // replicas), axis=1))
    inner = jnp.concatenate(full * (LANES // replicas), axis=0)
    row = lax.broadcasted_iota(jnp.int32, (LANES, LANES), 0)
    column = lax.broadcasted_iota(jnp.int32, (LANES, LANES), 1)

    def partner(values, stride, axis):
        place = column if axis else row
        ahead = pltpu.roll(values, stride, axis)
        behind = pltpu.roll(values, LANES - stride, axis)
        return jnp.where(place & stride != 0, ahead, behind)

    weight = jnp.ones((LANES, 1), jnp.float32)
    strides = [2**bit for bit in reversed(range(replicas.bit_length() - 2))] + [replicas // 2]
    for stride in strides:
        own = jnp.where(row == column, inner, 0.0)
        cross = jnp.where(row ^ stride == column, inner, 0.0)
        factors = []
        for axis in (1, 0):
            square = jnp.sum(own, axis=axis, keepdims=True)
            dot = jnp.sum(cross, axis=axis, keepdims=True)
            factors.append(1.0 - dot / (2.0 * (square + epsilon)))
        weight = weight * factors[0]
        scaled = factors[0] * inner * factors[1]
        scaled = scaled + partner(scaled, stride, 0)
        inner = scaled + partner(scaled, stride, 1)
    weight = weight[:replicas]
    for index in range(columns):
        total = jnp.sum(slices_ref[index].astype(jnp.float32) * weight, axis=0, keepdims=True)
        for part in range(rows // LANES):
            flat_ref[pl.ds(index * rows // LANES + part, 1), :] = total[
                :, part * LANES : (part + 1) * LANES
            ]
    flat = flat_ref[...].astype(jnp.bfloat16)
    for copy in range(sum_ref.shape[0]):
        sum_ref[copy] = flat


def combine(gram_matrix, slices):
    columns, replicas, rows = slices.shape
    height = columns * rows // LANES
    return pl.pallas_call(
        combine_kernel,
        out_shape=jax.ShapeDtypeStruct((replicas // 2, height, LANES), jnp.bfloat16),
        scratch_shapes=[pltpu.VMEM((height, LANES), jnp.float32)],
        name="combine",
    )(gram_matrix, slices)


def exchange(value, axis):
    return lax.all_to_all(value, axis, 0, 0, tiled=True)


def share(value, axis):
    members = lax.axis_size(axis)
    return exchange(jnp.broadcast_to(value, (members, *value.shape)), axis)


def sum_everywhere(halves):
    part = jnp.sum(exchange(halves, "core"), axis=0)
    part = jnp.sum(share(part, "z"), axis=0)
    part = jnp.sum(share(part, CHIPS), axis=0)
    return share(part, "core")


def update_kernel(
    first_row_ref,
    total_ref,
    features_ref,
    weights_ref,
    old_ref,
    momentum_ref,
    weights_out,
    momentum_out,
    flat_ref,
    rows_ref,
    adasum_ref,
):
    block, owned_rows = weights_out.shape[0], momentum_ref.shape[0]
    step = pl.program_id(0)
    first_row = first_row_ref[0]

    @pl.when(step == 0)
    def _():
        flat_ref[...] = total_ref[...].astype(jnp.float32).reshape(flat_ref.shape)
        height, width = rows_ref.shape
        parts = width // LANES
        for part in range(parts):
            rows_ref[:, part * LANES : (part + 1) * LANES] = flat_ref[
                pl.ds(part, height, stride=parts), :
            ].astype(jnp.bfloat16)

    adasum = lax.dot_general(
        features_ref[...],
        rows_ref[...],
        (((1,), (1,)), ((), ())),
        preferred_element_type=jnp.float32,
    )
    new_momentum = momentum_decay * old_ref[...].astype(jnp.float32) + adasum
    weights_out[...] = (
        weights_ref[...].astype(jnp.float32) - learning_rate * new_momentum
    ).astype(jnp.bfloat16)

    @pl.when(step == first_row // block)
    def _():
        adasum_ref[...] = adasum
        own = pl.ds(pl.multiple_of(first_row % block, 8), owned_rows)
        momentum_out[...] = momentum_decay * momentum_ref[...] + adasum_ref[own, :]


def update(first_row, total, features, weights, old_momentum, momentum):
    height, hidden = weights.shape
    rows = features.shape[1]
    block = 640
    blocked = pl.BlockSpec((block, hidden), lambda step, _: (step, 0))
    return pl.pallas_call(
        update_kernel,
        grid_spec=pltpu.PrefetchScalarGridSpec(
            num_scalar_prefetch=1,
            grid=(height // block,),
            in_specs=[
                pl.BlockSpec(total.shape, lambda step, _: (0, 0, 0, 0)),
                pl.BlockSpec((block, rows), lambda step, _: (step, 0)),
                blocked,
                blocked,
                pl.BlockSpec(momentum.shape, lambda step, _: (0, 0)),
            ],
            out_specs=(blocked, pl.BlockSpec(momentum.shape, lambda step, _: (0, 0))),
            scratch_shapes=[
                pltpu.VMEM((hidden * rows // LANES, LANES), jnp.float32),
                pltpu.VMEM((hidden, rows), jnp.bfloat16),
                pltpu.VMEM((block, hidden), jnp.float32),
            ],
        ),
        out_shape=(
            jax.ShapeDtypeStruct(weights.shape, jnp.bfloat16),
            jax.ShapeDtypeStruct(momentum.shape, jnp.float32),
        ),
        name="update",
    )(
        first_row.reshape(1),
        total,
        features,
        weights,
        old_momentum,
        momentum,
    )


def body(token_ids, table, weights, targets, momentum):
    replicas = lax.axis_size(REPLICAS)
    owned_rows, hidden = momentum.shape
    rows = table.shape[0]
    columns = hidden // replicas

    chosen = token_ids[:, None] == lax.broadcasted_iota(jnp.int32, (token_ids.shape[0], rows), 1)
    counts = jnp.sum(chosen.astype(jnp.float32), axis=0, keepdims=True)
    wanted = lax.dot_general(
        targets,
        chosen.astype(jnp.bfloat16),
        (((0,), (0,)), ((), ())),
        preferred_element_type=jnp.float32,
    )
    preact = lax.dot_general(
        weights, table, (((0,), (1,)), ((), ())), preferred_element_type=jnp.float32
    )
    activated, pullback = jax.vjp(gelu_tanh, preact)
    row_grads = pullback(counts * activated - wanted)[0].astype(jnp.bfloat16)

    row_grads, table, momentum = lax.optimization_barrier((row_grads, table, momentum))
    old_momentum = lax.all_gather(momentum.astype(jnp.bfloat16), REPLICAS, axis=0, tiled=True)
    slices = exchange(row_grads.reshape(replicas, columns * rows // LANES, LANES), CORES_FIRST)
    slices = slices.reshape(replicas, columns, rows).transpose(1, 0, 2)
    kernel = lax.dot_general(
        table, table, (((1,), (1,)), ((), ())), preferred_element_type=jnp.float32
    )
    total = combine(sum_everywhere(gram(slices, kernel)), slices)
    total = share(exchange(total, CHIPS), "core")
    first_row = lax.axis_index(REPLICAS) * owned_rows
    return update(first_row, total, table.T, weights, old_momentum, momentum)


def solution(mesh):
    axes = Mesh(mesh.devices.reshape(*FACTORS, -1), (*REPLICAS, "z"))
    placed = (P(REPLICAS), P(), P(None, "z"), P(REPLICAS, "z"), P(REPLICAS, "z"))
    return jax.shard_map(
        body,
        mesh=axes,
        in_specs=placed,
        out_specs=(P(None, "z"), P(REPLICAS, "z")),
        check_vma=False,
    )
```

time: 167 us -> 161 us (0.964)
  blocking collectives: 95.9 us -> 60 us
  starting transfers between devices: 6.36 us -> 23.8 us
  waiting for transfers between devices: 17.8 us -> 28 us
  Pallas kernels: 19.4 us -> 14.1 us
  local copies, waits for them, and re-layouts: 4.67 us -> 8.77 us
  matrix products: 6.14 us -> 9.49 us
    all_to_all x4 -> x5, blocking collectives: 95.9 us -> 60 us  [exchange(): return lax.all_to_all(value, axis, 0, 0, tiled=True)]
    all_to_all x1 -> x2, starting transfers between devices: 6.33 us -> 23.8 us  [exchange(): return lax.all_to_all(value, axis, 0, 0, tiled=True)]
    all_to_all x1 -> x2, waiting for transfers between devices: 17.8 us -> 28 us  [exchange(): return lax.all_to_all(value, axis, 0, 0, tiled=True)]
    pallas_call x2, Pallas kernels: 9.83 us -> 6.28 us  [the longest x1 3.2 us: gram(): pl.pallas_call(gram_kernel, out_shape=jax.ShapeDtypeStruct((2, replicas /...]
    optimization_barrier x0 -> x1, local copies, waits for them, and re-layouts: none -> 2.64 us  [body(): lax.optimization_barrier((row_grads, table, momentum))]
    unnamed x7 -> x10, local copies, waits for them, and re-layouts: 2.65 us -> 0.03 us
    dot_general x0 -> x1, matrix products: none -> 2.52 us  [body(): lax.dot_general(table, table, (((1,), (1,)), ((), ())), preferred_element...]
    reshape x1, local copies, waits for them, and re-layouts: 0.39 us -> 2.35 us  [body(): row_grads.reshape(replicas, columns * rows // LANES, LANES)]
  transfers between devices with their start and end apart: 2 -> 3, of which waited for: 1 -> 2; matrix products, arithmetic and copies ran while one was open for 7% -> 7% of each run, Pallas kernels for 6% -> 4%
where the time goes in v3:
time: 161 us; the launch traced here: 160 us
  blocking collectives  60 us (37%)
  waiting for transfers between devices  28 us (17%)
  starting transfers between devices  23.8 us (15%)
  between operations  14.2 us (9%)
  Pallas kernels  14.1 us (9%)
  matrix products  9.49 us (6%)
  local copies, waits for them, and re-layouts  8.77 us (5%)
    all_to_all x5, blocking collectives, exchange(): return lax.all_to_all(value, axis, 0, 0, tiled=True)  60 us
    all_to_all x2, waiting for transfers between devices, exchange(): return lax.all_to_all(value, axis, 0, 0, tiled=True)  28 us
    all_to_all x2, starting transfers between devices, exchange(): return lax.all_to_all(value, axis, 0, 0, tiled=True)  23.8 us
    pallas_call x1, Pallas kernels, update(): pl.pallas_call(update_kernel, grid_spec=pltpu.PrefetchScalarGridSpec(num_...  7.77 us
    dot_general x1, matrix products, body(): lax.dot_general(weights, table, (((0,), (1,)), ((), ())), preferred_eleme...  4.64 us
  transfers between devices with their start and end apart: 3, of which 2 were waited for; matrix products, arithmetic and copies ran while one was open for 7% of the time, Pallas kernels for 4%

profile of v3, /device:TPU:1, one launch (start us, length us, event | category | flops | bytes accessed | tf_op | source)
XLA Modules:
  0.0 159.9 jit_solution(5712321183530292979)
XLA Ops:
  7.2 0.0 copy-start
  7.2 0.0 all-gather.2.cloned.1.call-start
  7.2 0.9 convert_reduce_fusion
  8.1 0.0 copy-start.4
  8.2 4.6 %fusion.9 = f32[640,512]{1,0:T(8,128)S(1)} fusion(bf16[2560,640]{1,0:T(8,128)(2,1)} %weights_ref.1, bf16[512,2560]{1,0:T(8,128)(2,1)} %param.6), kind=kOutput, calls=%fused_computation.15 | convolution fusion | flops 1677721600 | bytes 7208960 | tf_op jit(solution)/shard_map/dot_general | solution.py:228
  12.8 0.0 copy-done
  12.8 0.0 copy-done.4
  12.8 0.0 copy-start.3
  12.8 2.3 %fusion.7 = bf16[640,512]{1,0:T(8,128)(2,1)} fusion(f32[640,512]{1,0:T(8,128)S(1)} %fusion.9, bf16[512,640]{1,0:T(8,128)(2,1)S(1)} %copy-done, f32[512]{0:T(512)S(1)} %convert_reduce_fusion, s32[512]{0:T(512)S(1)} %copy-done.4), kind=kOutput, calls=%fused_computation.10 | convolution fusion | flops 343343104 | bytes 2625536 | tf_op jit(solution)/shard_map/dot_general | solution.py:222
  15.2 0.0 copy-done.3
  15.2 0.6 convert_element_type.12
  15.8 0.0 copy-start.1
  15.8 0.0 all-gather.2.cloned.1.call-update
  15.8 2.4 %reshape.16 = bf16[64,40,128]{2,1,0:T(8,128)(2,1)} reshape(bf16[640,512]{1,0:T(8,128)(2,1)} %fusion.7) | data formatting | bytes 1310720 | tf_op jit(solution)/shard_map/reshape | solution.py:236
  18.2 19.2 %all-to-all-start = ((bf16[64,40,128]{2,1,0:T(8,128)(2,1)}), bf16[64,40,128]{2,1,0:T(8,128)(2,1)}, u32[]{:S(2)}, u32[]{:S(2)}) async-start(bf16[64,40,128]{2,1,0:T(8,128)(2,1)} %reshape.16), calls=%async_computation | async-start | bytes 1310720 | tf_op jit(solution)/shard_map/all_to_all | solution.py:115
  37.3 0.0 copy-done.1
  37.4 2.5 %fusion.10.kernel_ref = f32[512,512]{1,0:T(8,128)} fusion(bf16[512,2560]{1,0:T(8,128)(2,1)S(1)} %copy-done.1), kind=kOutput, calls=%fused_computation.16 | convolution fusion | flops 1342177280 | bytes 3670016 | tf_op jit(solution)/shard_map/dot_general | solution.py:238
  39.9 17.8 %all-to-all-done = bf16[64,40,128]{2,1,0:T(8,128)(2,1)} async-done(((bf16[64,40,128]{2,1,0:T(8,128)(2,1)}), bf16[64,40,128]{2,1,0:T(8,128)(2,1)}, u32[]{:S(2)}, u32[]{:S(2)}) %all-to-all-start) | async-done | bytes 655392 | tf_op jit(solution)/shard_map/all_to_all | solution.py:115
  57.7 1.4 reshape.17
  59.2 1.2 copy.17
  60.4 3.2 %gram.1 = f32[2,16,128]{2,1,0:T(8,128)} custom-call(bf16[10,64,512]{2,1,0:T(8,128)(2,1)} %bitcast.17, f32[512,512]{1,0:T(8,128)} %fusion.10.kernel_ref), custom_call_target="tpu_custom_call" | custom-call | tf_op jit(solution)/shard_map/gram/pallas_call | solution.py:53
  63.6 4.3 %all_to_all.35 = f32[2,16,128]{2,1,0:T(8,128)S(1)} all-to-all(f32[2,16,128]{2,1,0:T(8,128)} %gram.1), channel_id=1, replica_groups=mesh['y'=8,'x'=4,'core'=2,'z'=16] {'core'}, dimensions={0} | all-to-all | bytes 32768 | tf_op jit(solution)/shard_map/all_to_all | solution.py:115
  67.8 23.3 %all_to_all.36 = f32[16,16,128]{2,1,0:T(8,128)S(1)} all-to-all(f32[16,16,128]{2,1,0:T(8,128)S(1)} %broadcast_in_dim.14), channel_id=1, replica_groups=mesh['y'=8,'x'=4,'core'=2,'z'=16] {'z'}, dimensions={0} | all-to-all | bytes 262144 | tf_op jit(solution)/shard_map/all_to_all | solution.py:115
  91.2 0.0 copy-start.2
  91.2 17.1 %all_to_all.37 = f32[32,16,128]{2,1,0:T(8,128)S(1)} all-to-all(f32[32,16,128]{2,1,0:T(8,128)S(1)} %broadcast_in_dim.15), channel_id=1, replica_groups=mesh['y'=8,'x'=4,'core'=2,'z'=16] {'y','x'}, dimensions={0} | all-to-all | bytes 524288 | tf_op jit(solution)/shard_map/all_to_all | solution.py:115
  108.4 8.4 %all_to_all.38.gram_ref = f32[2,16,128]{2,1,0:T(8,128)} all-to-all(f32[2,16,128]{2,1,0:T(8,128)S(1)} %broadcast_in_dim.16), channel_id=1, replica_groups=mesh['y'=8,'x'=4,'core'=2,'z'=16] {'core'}, dimensions={0} | all-to-all | bytes 32768 | tf_op jit(solution)/shard_map/all_to_all | solution.py:115
  116.8 3.1 %combine.1 = bf16[32,40,128]{2,1,0:T(8,128)(2,1)} custom-call(f32[2,16,128]{2,1,0:T(8,128)} %all_to_all.38.gram_ref, bf16[10,64,512]{2,1,0:T(8,128)(2,1)} %bitcast.18), custom_call_target="tpu_custom_call" | custom-call | tf_op jit(solution)/shard_map/combine/pallas_call | solution.py:106
  119.8 4.6 %all-to-all-start.5 = ((bf16[32,40,128]{2,1,0:T(8,128)(2,1)}), bf16[32,40,128]{2,1,0:T(8,128)(2,1)}, u32[]{:S(2)}, u32[]{:S(2)}) async-start(bf16[32,40,128]{2,1,0:T(8,128)(2,1)} %combine.1), calls=%async_computation.5 | async-start | bytes 655360 | tf_op jit(solution)/shard_map/all_to_all | solution.py:115
  124.4 0.0 copy-done.2
  124.4 2.6 %copy.14 = bf16[512,2560]{0,1:T(8,128)(2,1)} copy(bf16[512,2560]{1,0:T(8,128)(2,1)S(1)} %copy-done.2) | data formatting | bytes 5242880 | tf_op jit(solution)/shard_map/optimization_barrier | solution.py:234
  127.1 10.2 %all-to-all-done.5 = bf16[32,40,128]{2,1,0:T(8,128)(2,1)} async-done(((bf16[32,40,128]{2,1,0:T(8,128)(2,1)}), bf16[32,40,128]{2,1,0:T(8,128)(2,1)}, u32[]{:S(2)}, u32[]{:S(2)}) %all-to-all-start.5) | async-done | bytes 327712 | tf_op jit(solution)/shard_map/all_to_all | solution.py:115
  137.3 1.1 broadcast_in_dim.17
  138.3 6.9 %all_to_all.39.total_ref = bf16[2,32,40,128]{3,2,1,0:T(8,128)(2,1)} all-to-all(bf16[2,32,40,128]{3,2,1,0:T(8,128)(2,1)S(1)} %broadcast_in_dim.17), channel_id=1, replica_groups=mesh['y'=8,'x'=4,'core'=2,'z'=16] {'core'}, dimensions={0} | all-to-all | bytes 1310720 | tf_op jit(solution)/shard_map/all_to_all | solution.py:115
  145.3 0.0 all-gather.2.cloned.1.call-done.old_ref
  145.3 7.8 %update.1 = (bf16[2560,640]{1,0:T(8,128)(2,1)}, f32[40,640]{1,0:T(8,128)}) custom-call(s32[1]{0:T(128)} %bitcast.first_row_ref, bf16[2,32,40,128]{3,2,1,0:T(8,128)(2,1)} %all_to_all.39.total_ref, bf16[2560,512]{1,0:T(8,128)(2,1)} %bitcast.16, bf16[2560,640]{1,0:T(8,128)(2,1)} %weights_ref.1, bf16[2560,640]{1,0:T(8,128)(2,1)} %all-gather.2.cloned.1.call-done.old_ref, ...), custom_call_target="tpu_custom_call" | custom-call | tf_op jit(solution)/shard_map/update/pallas_call | solution.py:180
  (6 shorter events, 0.1 us)
Async XLA Ops:
  7.2 5.6 %copy-start = (bf16[512,640]{1,0:T(8,128)(2,1)S(1)}, bf16[512,640]{1,0:T(8,128)(2,1)}, u32[]{:S(2)}) copy-start(bf16[512,640]{1,0:T(8,128)(2,1)} %param.8) | copy-start | bytes 1966084
  7.2 138.1 %all-gather.2.cloned.1.call-start = ((), (), s32[]{:S(2)}) async-start(), calls=%async_computation.7 | async-start | bytes 3328000 | tf_op jit(solution)/shard_map/all_gather | solution.py:235
  8.1 4.7 %copy-start.4 = (s32[512]{0:T(512)S(1)}, s32[512]{0:T(512)}, u32[]{:S(2)}) copy-start(s32[512]{0:T(512)} %param.5) | copy-start | bytes 6148
  12.8 2.3 %copy-start.3 = (f32[40,640]{1,0:T(8,128)S(1)}, f32[40,640]{1,0:T(8,128)}, u32[]{:S(2)}) copy-start(f32[40,640]{1,0:T(8,128)} %momentum_ref) | copy-start | bytes 307204
  15.8 21.6 %copy-start.1 = (bf16[512,2560]{1,0:T(8,128)(2,1)S(1)}, bf16[512,2560]{1,0:T(8,128)(2,1)}, u32[]{:S(2)}) copy-start(bf16[512,2560]{1,0:T(8,128)(2,1)} %param.6) | copy-start | bytes 7864324
  18.2 39.5 %all-to-all-start = ((bf16[64,40,128]{2,1,0:T(8,128)(2,1)}), bf16[64,40,128]{2,1,0:T(8,128)(2,1)}, u32[]{:S(2)}, u32[]{:S(2)}) async-start(bf16[64,40,128]{2,1,0:T(8,128)(2,1)} %reshape.16), calls=%async_computation | async-start | bytes 1310720 | tf_op jit(solution)/shard_map/all_to_all | solution.py:115
  91.2 33.2 %copy-start.2 = (bf16[512,2560]{1,0:T(8,128)(2,1)S(1)}, bf16[512,2560]{1,0:T(8,128)(2,1)}, u32[]{:S(2)}) copy-start(bf16[512,2560]{1,0:T(8,128)(2,1)} %param.6) | copy-start | bytes 7864324
  119.8 17.4 %all-to-all-start.5 = ((bf16[32,40,128]{2,1,0:T(8,128)(2,1)}), bf16[32,40,128]{2,1,0:T(8,128)(2,1)}, u32[]{:S(2)}, u32[]{:S(2)}) async-start(bf16[32,40,128]{2,1,0:T(8,128)(2,1)} %combine.1), calls=%async_computation.5 | async-start | bytes 655360 | tf_op jit(solution)/shard_map/all_to_all | solution.py:115
Sparse Core Ops, SparseCore 0:
  15.9 104.2 all-gather.1

commit v4 on v3

--- a/solution.py
+++ b/solution.py
@@ -21,9 +21,46 @@
     return jax.nn.gelu(values, approximate=True)
 
 
-def gram_kernel(slices_ref, kernel_ref, gram_ref):
-    columns, replicas, rows = slices_ref.shape
-    values = slices_ref[...].reshape(columns * replicas, rows)
+def rows_kernel(ids_ref, preact_ref, targets_ref, blocks_ref, flat_ref):
+    hidden, rows = preact_ref.shape
+    tokens = targets_ref.shape[0]
+    parts = rows // LANES
+    targets = targets_ref[...].T
+    ones = jnp.ones((8, tokens), jnp.bfloat16)
+    over_tokens = (((1,), (1,)), ((), ()))
+    for part in range(parts):
+        row = part * LANES + lax.broadcasted_iota(jnp.int32, (LANES, tokens), 0)
+        chosen = (row == ids_ref[...]).astype(jnp.float32).astype(jnp.bfloat16)
+        counts = lax.dot_general(ones, chosen, over_tokens, preferred_element_type=jnp.float32)
+        wanted = lax.dot_general(targets, chosen, over_tokens, preferred_element_type=jnp.float32)
+        preact = preact_ref[:, part * LANES : (part + 1) * LANES]
+        activated, pullback = jax.vjp(gelu_tanh, preact)
+        flat_ref[pl.ds(part, hidden, stride=parts), :] = pullback(counts[:1] * activated - wanted)[0]
+    blocks_ref[...] = flat_ref[...].reshape(blocks_ref.shape).astype(jnp.bfloat16)
+
+
+def row_blocks(token_ids, preact, targets, replicas):
+    hidden, rows = preact.shape
+    height = hidden * rows // LANES
+    return pl.pallas_call(
+        rows_kernel,
+        out_shape=jax.ShapeDtypeStruct((replicas, height // replicas, LANES), jnp.bfloat16),
+        scratch_shapes=[pltpu.VMEM((height, LANES), jnp.float32)],
+        name="rows",
+    )(token_ids.reshape(1, -1), preact, targets)
+
+
+def gram_kernel(blocks_ref, kernel_ref, gram_ref, flat_ref, values_ref):
+    replicas, height, _ = blocks_ref.shape
+    rows = kernel_ref.shape[0]
+    parts = rows // LANES
+    flat_ref[...] = blocks_ref[...].astype(jnp.float32).reshape(flat_ref.shape)
+    for index in range(height):
+        column, part = index // parts, index % parts
+        values_ref[
+            column * replicas : (column + 1) * replicas, part * LANES : (part + 1) * LANES
+        ] = flat_ref[pl.ds(index, replicas, stride=height), :].astype(jnp.bfloat16)
+    values = values_ref[...]
     high = kernel_ref[...].astype(jnp.bfloat16)
     low = (kernel_ref[...] - high.astype(jnp.float32)).astype(jnp.bfloat16)
     images = (
@@ -31,7 +68,7 @@
         + jnp.dot(values, low, preferred_element_type=jnp.float32)
     ).astype(jnp.bfloat16)
     total = jnp.zeros((replicas, replicas), jnp.float32)
-    for start in range(0, columns * replicas, WIDE):
+    for start in range(0, values.shape[0], WIDE):
         products = lax.dot_general(
             values[start : start + WIDE],
             images[start : start + WIDE],
@@ -40,29 +77,36 @@
         )
         for own in range(0, products.shape[0], replicas):
             total += products[own : own + replicas, own : own + replicas]
-    height = replicas // 4
+    lines = replicas // 4
     for half in range(2):
-        first = 2 * half * height
+        first = 2 * half * lines
         gram_ref[half] = jnp.concatenate(
-            [total[first : first + height], total[first + height : first + 2 * height]], axis=1
+            [total[first : first + lines], total[first + lines : first + 2 * lines]], axis=1
         )
 
 
-def gram(slices, kernel):
-    replicas = slices.shape[1]
+def gram(blocks, kernel):
+    replicas, height, _ = blocks.shape
+    rows = kernel.shape[0]
     return pl.pallas_call(
         gram_kernel,
         out_shape=jax.ShapeDtypeStruct((2, replicas // 4, 2 * replicas), jnp.float32),
+        scratch_shapes=[
+            pltpu.VMEM((replicas * height, LANES), jnp.float32),
+            pltpu.VMEM((replicas * height * LANES // rows, rows), jnp.bfloat16),
+        ],
         name="gram",
-    )(slices, kernel)
-
-
-def combine_kernel(gram_ref, slices_ref, sum_ref, flat_ref):
-    columns, replicas, rows = slices_ref.shape
+    )(blocks, kernel)
+
+
+def combine_kernel(gram_ref, blocks_ref, sum_ref, weight_ref):
+    replicas, height, _ = blocks_ref.shape
+    chips = gram_ref.shape[0] // 2
+    halves = [jnp.sum(gram_ref[half * chips : (half + 1) * chips], axis=0) for half in range(2)]
     full = []
     for half in range(2):
         for side in range(2):
-            lines = gram_ref[half, :, side * replicas : (side + 1) * replicas]
+            lines = halves[half][:, side * replicas : (side + 1) * replicas]
             full.append(jnp.concatenate([lines] * (LANES // replicas), axis=1))
     inner = jnp.concatenate(full * (LANES // replicas), axis=0)
     row = lax.broadcasted_iota(jnp.int32, (LANES, LANES), 0)
@@ -88,27 +132,23 @@
         scaled = factors[0] * inner * factors[1]
         scaled = scaled + partner(scaled, stride, 0)
         inner = scaled + partner(scaled, stride, 1)
-    weight = weight[:replicas]
-    for index in range(columns):
-        total = jnp.sum(slices_ref[index].astype(jnp.float32) * weight, axis=0, keepdims=True)
-        for part in range(rows // LANES):
-            flat_ref[pl.ds(index * rows // LANES + part, 1), :] = total[
-                :, part * LANES : (part + 1) * LANES
-            ]
-    flat = flat_ref[...].astype(jnp.bfloat16)
+    weight_ref[...] = jnp.broadcast_to(weight, weight_ref.shape)
+    total = jnp.zeros((height, LANES), jnp.float32)
+    for replica in range(replicas):
+        total += blocks_ref[replica].astype(jnp.float32) * weight_ref[pl.ds(replica, 1), :]
+    total = total.astype(jnp.bfloat16)
     for copy in range(sum_ref.shape[0]):
-        sum_ref[copy] = flat
-
-
-def combine(gram_matrix, slices):
-    columns, replicas, rows = slices.shape
-    height = columns * rows // LANES
+        sum_ref[copy] = total
+
+
+def combine(gram_parts, blocks):
+    replicas, height, _ = blocks.shape
     return pl.pallas_call(
         combine_kernel,
         out_shape=jax.ShapeDtypeStruct((replicas // 2, height, LANES), jnp.bfloat16),
-        scratch_shapes=[pltpu.VMEM((height, LANES), jnp.float32)],
+        scratch_shapes=[pltpu.VMEM((LANES, LANES), jnp.float32)],
         name="combine",
-    )(gram_matrix, slices)
+    )(gram_parts, blocks)
 
 
 def exchange(value, axis):
@@ -120,16 +160,10 @@
     return exchange(jnp.broadcast_to(value, (members, *value.shape)), axis)
 
 
-def sum_everywhere(halves):
-    part = jnp.sum(exchange(halves, "core"), axis=0)
-    part = jnp.sum(share(part, "z"), axis=0)
-    part = jnp.sum(share(part, CHIPS), axis=0)
-    return share(part, "core")
-
-
 def update_kernel(
-    first_row_ref,
-    total_ref,
+    place_ref,
+    own_ref,
+    other_ref,
     features_ref,
     weights_ref,
     old_ref,
@@ -142,11 +176,15 @@
 ):
     block, owned_rows = weights_out.shape[0], momentum_ref.shape[0]
     step = pl.program_id(0)
-    first_row = first_row_ref[0]
+    first_row = place_ref[0]
 
     @pl.when(step == 0)
     def _():
-        flat_ref[...] = total_ref[...].astype(jnp.float32).reshape(flat_ref.shape)
+        half = flat_ref.shape[0] // 2
+        for blocks_ref, core in ((own_ref, place_ref[1]), (other_ref, 1 - place_ref[1])):
+            flat_ref[pl.ds(pl.multiple_of(core * half, half), half), :] = (
+                blocks_ref[...].astype(jnp.float32).reshape(half, LANES)
+            )
         height, width = rows_ref.shape
         parts = width // LANES
         for part in range(parts):
@@ -172,7 +210,7 @@
         momentum_out[...] = momentum_decay * momentum_ref[...] + adasum_ref[own, :]
 
 
-def update(first_row, total, features, weights, old_momentum, momentum):
+def update(place, own, other, features, weights, old_momentum, momentum):
     height, hidden = weights.shape
     rows = features.shape[1]
     block = 640
@@ -183,7 +221,8 @@
             num_scalar_prefetch=1,
             grid=(height // block,),
             in_specs=[
-                pl.BlockSpec(total.shape, lambda step, _: (0, 0, 0, 0)),
+                pl.BlockSpec(own.shape, lambda step, _: (0, 0, 0)),
+                pl.BlockSpec(own.shape, lambda step, _: (0, 0, 0)),
                 pl.BlockSpec((block, rows), lambda step, _: (step, 0)),
                 blocked,
                 blocked,
@@ -202,8 +241,9 @@
         ),
         name="update",
     )(
-        first_row.reshape(1),
-        total,
+        place,
+        own,
+        other,
         features,
         weights,
         old_momentum,
@@ -214,34 +254,22 @@
 def body(token_ids, table, weights, targets, momentum):
     replicas = lax.axis_size(REPLICAS)
     owned_rows, hidden = momentum.shape
-    rows = table.shape[0]
-    columns = hidden // replicas
-
-    chosen = token_ids[:, None] == lax.broadcasted_iota(jnp.int32, (token_ids.shape[0], rows), 1)
-    counts = jnp.sum(chosen.astype(jnp.float32), axis=0, keepdims=True)
-    wanted = lax.dot_general(
-        targets,
-        chosen.astype(jnp.bfloat16),
-        (((0,), (0,)), ((), ())),
-        preferred_element_type=jnp.float32,
-    )
     preact = lax.dot_general(
         weights, table, (((0,), (1,)), ((), ())), preferred_element_type=jnp.float32
     )
-    activated, pullback = jax.vjp(gelu_tanh, preact)
-    row_grads = pullback(counts * activated - wanted)[0].astype(jnp.bfloat16)
-
-    row_grads, table, momentum = lax.optimization_barrier((row_grads, table, momentum))
+    blocks = row_blocks(token_ids, preact, targets, replicas)
+    blocks, table, momentum = lax.optimization_barrier((blocks, table, momentum))
     old_momentum = lax.all_gather(momentum.astype(jnp.bfloat16), REPLICAS, axis=0, tiled=True)
-    slices = exchange(row_grads.reshape(replicas, columns * rows // LANES, LANES), CORES_FIRST)
-    slices = slices.reshape(replicas, columns, rows).transpose(1, 0, 2)
+    blocks = exchange(blocks, CORES_FIRST)
     kernel = lax.dot_general(
         table, table, (((1,), (1,)), ((), ())), preferred_element_type=jnp.float32
     )
-    total = combine(sum_everywhere(gram(slices, kernel)), slices)
-    total = share(exchange(total, CHIPS), "core")
-    first_row = lax.axis_index(REPLICAS) * owned_rows
-    return update(first_row, total, table.T, weights, old_momentum, momentum)
+    part = jnp.sum(exchange(gram(blocks, kernel), "core"), axis=0)
+    part = jnp.sum(share(part, "z"), axis=0)
+    own = exchange(combine(share(part, CORES_FIRST), blocks), CHIPS)
+    other = lax.ppermute(own, "core", [(0, 1), (1, 0)])
+    place = jnp.stack([lax.axis_index(REPLICAS) * owned_rows, lax.axis_index("core")])
+    return update(place, own, other, table.T, weights, old_momentum, momentum)
 
 
 def solution(mesh):

time: 161 us -> 165 us (1.025)
  blocking collectives: 60 us -> 76.9 us
  waiting for transfers between devices: 28 us -> 17.7 us
  Pallas kernels: 14.1 us -> 18.8 us
  local copies, waits for them, and re-layouts: 8.77 us -> 4.29 us
    all_to_all x5 -> x4, blocking collectives: 60 us -> 76.9 us  [exchange(): return lax.all_to_all(value, axis, 0, 0, tiled=True)]
    all_to_all x2 -> x1, waiting for transfers between devices: 28 us -> 17.7 us  [exchange(): return lax.all_to_all(value, axis, 0, 0, tiled=True)]
    all_to_all x2 -> x1, starting transfers between devices: 23.8 us -> 18.4 us  [exchange(): return lax.all_to_all(value, axis, 0, 0, tiled=True)]
    reshape x3 -> x0, local copies, waits for them, and re-layouts: 5 us -> none  [the longest x2 2.65 us: body(): slices = slices.reshape(replicas, columns, rows).transpose(1, 0, 2)]
    ppermute x0 -> x1, starting transfers between devices: none -> 4.31 us  [body(): other = lax.ppermute(own, 'core', [(0, 1), (1, 0)])]
    pallas_call x0 -> x1, Pallas kernels: none -> 3.83 us  [row_blocks(): pl.pallas_call(rows_kernel, out_shape=jax.ShapeDtypeStruct((replicas, hei...]
    dot_general x1 -> x0, matrix products: 2.33 us -> none  [body(): lax.dot_general(targets, chosen.astype(jnp.bfloat16), (((0,), (0,)), ((),...]
  transfers between devices with their start and end apart: 3 -> 3, of which waited for: 2 -> 1; matrix products, arithmetic and copies ran while one was open for 7% -> 4% of each run, Pallas kernels for 4% -> 4%
where the time goes in v4:
time: 165 us; the launch traced here: 164 us
  blocking collectives  76.9 us (47%)
  starting transfers between devices  22.8 us (14%)
  Pallas kernels  18.8 us (11%)
  waiting for transfers between devices  17.7 us (11%)
  between operations  14.1 us (9%)
  matrix products  8.25 us (5%)
  local copies, waits for them, and re-layouts  4.29 us (3%)
    all_to_all x4, blocking collectives, exchange(): return lax.all_to_all(value, axis, 0, 0, tiled=True)  76.9 us
    all_to_all x1, starting transfers between devices, exchange(): return lax.all_to_all(value, axis, 0, 0, tiled=True)  18.4 us
    all_to_all x1, waiting for transfers between devices, exchange(): return lax.all_to_all(value, axis, 0, 0, tiled=True)  17.7 us
    pallas_call x1, Pallas kernels, update(): pl.pallas_call(update_kernel, grid_spec=pltpu.PrefetchScalarGridSpec(num_...  8.43 us
    dot_general x1, matrix products, body(): lax.dot_general(weights, table, (((0,), (1,)), ((), ())), preferred_eleme...  5.73 us
    ppermute x1, starting transfers between devices, body(): other = lax.ppermute(own, 'core', [(0, 1), (1, 0)])  4.31 us
    pallas_call x1, Pallas kernels, row_blocks(): pl.pallas_call(rows_kernel, out_shape=jax.ShapeDtypeStruct((replicas, hei...  3.83 us
    pallas_call x1, Pallas kernels, gram(): pl.pallas_call(gram_kernel, out_shape=jax.ShapeDtypeStruct((2, replicas /...  3.35 us
  transfers between devices with their start and end apart: 3, of which 1 were waited for; matrix products, arithmetic and copies ran while one was open for 4% of the time, Pallas kernels for 4%

profile of v4, /device:TPU:1, one launch (start us, length us, event | category | flops | bytes accessed | tf_op | source)
XLA Modules:
  0.0 164.0 jit_solution(7877208138830618240)
XLA Ops:
  7.2 0.0 all-gather.2.cloned.1.call-start
  7.2 0.0 copy-start.3
  7.2 5.7 %fusion.preact_ref = f32[640,512]{1,0:T(8,128)} fusion(bf16[2560,640]{1,0:T(8,128)(2,1)} %weights_ref.1, bf16[512,2560]{1,0:T(8,128)(2,1)} %param.6), kind=kOutput, calls=%fused_computation.1 | convolution fusion | flops 1677721600 | bytes 7208960 | tf_op jit(solution)/shard_map/dot_general | solution.py:257
  12.9 0.0 copy-start.1
  12.9 3.8 %rows.1 = bf16[64,40,128]{2,1,0:T(8,128)(2,1)} custom-call(s32[1,512]{1,0:T(1,128)} %bitcast.9, f32[640,512]{1,0:T(8,128)} %fusion.preact_ref, bf16[512,640]{1,0:T(8,128)(2,1)} %targets_ref.1), custom_call_target="tpu_custom_call" | custom-call | tf_op jit(solution)/shard_map/rows/pallas_call | solution.py:45
  16.8 0.0 copy-done.3
  16.8 0.6 convert_element_type.3
  17.4 0.0 all-gather.2.cloned.1.call-update
  17.4 18.4 %all-to-all-start = ((bf16[64,40,128]{2,1,0:T(8,128)(2,1)}), bf16[64,40,128]{2,1,0:T(8,128)(2,1)S(1)}, u32[]{:S(2)}, u32[]{:S(2)}) async-start(bf16[64,40,128]{2,1,0:T(8,128)(2,1)} %rows.1), calls=%async_computation | async-start | bytes 1310720 | tf_op jit(solution)/shard_map/all_to_all | solution.py:155
  35.8 0.0 copy-done.1
  35.9 2.5 %fusion.1.kernel_ref = f32[512,512]{1,0:T(8,128)} fusion(bf16[512,2560]{1,0:T(8,128)(2,1)S(1)} %copy-done.1), kind=kOutput, calls=%fused_computation.2 | convolution fusion | flops 1342177280 | bytes 3670016 | tf_op jit(solution)/shard_map/dot_general | solution.py:264
  38.4 17.7 %all-to-all-done.blocks_ref = bf16[64,40,128]{2,1,0:T(8,128)(2,1)S(1)} async-done(((bf16[64,40,128]{2,1,0:T(8,128)(2,1)}), bf16[64,40,128]{2,1,0:T(8,128)(2,1)S(1)}, u32[]{:S(2)}, u32[]{:S(2)}) %all-to-all-start) | async-done | bytes 655392 | tf_op jit(solution)/shard_map/all_to_all | solution.py:155
  56.1 0.0 copy-start
  56.1 0.8 copy-done
  56.9 3.4 %gram.1 = f32[2,16,128]{2,1,0:T(8,128)} custom-call(bf16[64,40,128]{2,1,0:T(8,128)(2,1)} %copy-done, f32[512,512]{1,0:T(8,128)} %fusion.1.kernel_ref), custom_call_target="tpu_custom_call" | custom-call | tf_op jit(solution)/shard_map/gram/pallas_call | solution.py:91
  60.3 4.3 %all_to_all.25 = f32[2,16,128]{2,1,0:T(8,128)S(1)} all-to-all(f32[2,16,128]{2,1,0:T(8,128)} %gram.1), channel_id=1, replica_groups=mesh['y'=8,'x'=4,'core'=2,'z'=16] {'core'}, dimensions={0} | all-to-all | bytes 32768 | tf_op jit(solution)/shard_map/all_to_all | solution.py:155
  64.6 24.0 %all_to_all.26 = f32[16,16,128]{2,1,0:T(8,128)S(1)} all-to-all(f32[16,16,128]{2,1,0:T(8,128)S(1)} %broadcast_in_dim.6), channel_id=1, replica_groups=mesh['y'=8,'x'=4,'core'=2,'z'=16] {'z'}, dimensions={0} | all-to-all | bytes 262144 | tf_op jit(solution)/shard_map/all_to_all | solution.py:155
  88.6 31.2 %all_to_all.27.gram_ref = f32[64,16,128]{2,1,0:T(8,128)} all-to-all(f32[64,16,128]{2,1,0:T(8,128)S(1)} %broadcast_in_dim.7), channel_id=1, replica_groups=mesh['y'=8,'x'=4,'core'=2,'z'=16] {'core','y','x'}, dimensions={0} | all-to-all | bytes 1048576 | tf_op jit(solution)/shard_map/all_to_all | solution.py:155
  119.9 3.2 %combine.1 = bf16[32,40,128]{2,1,0:T(8,128)(2,1)} custom-call(f32[64,16,128]{2,1,0:T(8,128)} %all_to_all.27.gram_ref, bf16[64,40,128]{2,1,0:T(8,128)(2,1)} %copy-done), custom_call_target="tpu_custom_call" | custom-call | tf_op jit(solution)/shard_map/combine/pallas_call | solution.py:146
  123.1 17.4 %all_to_all.28.own_ref = bf16[32,40,128]{2,1,0:T(8,128)(2,1)S(1)} all-to-all(bf16[32,40,128]{2,1,0:T(8,128)(2,1)} %combine.1), channel_id=1, replica_groups=mesh['y'=8,'x'=4,'core'=2,'z'=16] {'y','x'}, dimensions={0} | all-to-all | bytes 655360 | tf_op jit(solution)/shard_map/all_to_all | solution.py:155
  140.5 0.0 copy-start.2
  140.5 4.3 %collective-permute-start = (bf16[32,40,128]{2,1,0:T(8,128)(2,1)S(1)}, bf16[32,40,128]{2,1,0:T(8,128)(2,1)S(1)}, u32[]{:S(2)}, u32[]{:S(2)}) collective-permute-start(bf16[32,40,128]{2,1,0:T(8,128)(2,1)S(1)} %all_to_all.28.own_ref), channel_id=1, source_target_pairs={{0,16},{16,0},{1,17},{17,1},{2,18},{18,2},{3,19},{19,3},{4,20},{20... | collective-permute-start | bytes 983048 | tf_op jit(solution)/shard_map/ppermute | solution.py:270
  144.8 2.7 %copy.8 = bf16[512,2560]{0,1:T(8,128)(2,1)} copy(bf16[512,2560]{1,0:T(8,128)(2,1)S(1)} %copy-done.1) | data formatting | bytes 5242880 | tf_op jit(solution)/shard_map/optimization_barrier | solution.py:261
  147.4 0.0 copy-done.2
  147.5 0.6 pad_add_fusion.place_ref
  148.0 0.0 collective-permute-done.other_ref
  148.0 0.0 copy-start.4
  148.0 0.0 all-gather.2.cloned.1.call-done.old_ref
  148.0 0.7 copy-done.4
  148.8 8.4 %update.1 = (bf16[2560,640]{1,0:T(8,128)(2,1)}, f32[40,640]{1,0:T(8,128)}) custom-call(s32[2]{0:T(128)} %pad_add_fusion.place_ref, bf16[32,40,128]{2,1,0:T(8,128)(2,1)} %copy-done.2, bf16[32,40,128]{2,1,0:T(8,128)(2,1)} %copy-done.4, bf16[2560,512]{1,0:T(8,128)(2,1)} %bitcast.8, bf16[2560,640]{1,0:T(8,128)(2,1)} %weights_ref.1, ...), custom_call_target="tpu_custom_call" | custom-call | tf_op jit(solution)/shard_map/update/pallas_call | solution.py:218
  (4 shorter events, 0.1 us)
Async XLA Ops:
  7.2 140.9 %all-gather.2.cloned.1.call-start = ((), (), s32[]{:S(2)}) async-start(), calls=%async_computation.5 | async-start | bytes 3328000 | tf_op jit(solution)/shard_map/all_gather | solution.py:262
  7.2 9.6 %copy-start.3 = (f32[40,640]{1,0:T(8,128)S(1)}, f32[40,640]{1,0:T(8,128)}, u32[]{:S(2)}) copy-start(f32[40,640]{1,0:T(8,128)} %momentum_ref) | copy-start | bytes 307204
  12.9 22.9 %copy-start.1 = (bf16[512,2560]{1,0:T(8,128)(2,1)S(1)}, bf16[512,2560]{1,0:T(8,128)(2,1)}, u32[]{:S(2)}) copy-start(bf16[512,2560]{1,0:T(8,128)(2,1)} %param.6) | copy-start | bytes 7864324
  17.4 38.7 %all-to-all-start = ((bf16[64,40,128]{2,1,0:T(8,128)(2,1)}), bf16[64,40,128]{2,1,0:T(8,128)(2,1)S(1)}, u32[]{:S(2)}, u32[]{:S(2)}) async-start(bf16[64,40,128]{2,1,0:T(8,128)(2,1)} %rows.1), calls=%async_computation | async-start | bytes 1310720 | tf_op jit(solution)/shard_map/all_to_all | solution.py:155
  56.1 0.8 copy-start
  140.5 7.0 %copy-start.2 = (bf16[32,40,128]{2,1,0:T(8,128)(2,1)}, bf16[32,40,128]{2,1,0:T(8,128)(2,1)S(1)}, u32[]{:S(2)}) copy-start(bf16[32,40,128]{2,1,0:T(8,128)(2,1)S(1)} %all_to_all.28.own_ref) | copy-start | bytes 983044
  140.5 7.6 %collective-permute-start = (bf16[32,40,128]{2,1,0:T(8,128)(2,1)S(1)}, bf16[32,40,128]{2,1,0:T(8,128)(2,1)S(1)}, u32[]{:S(2)}, u32[]{:S(2)}) collective-permute-start(bf16[32,40,128]{2,1,0:T(8,128)(2,1)S(1)} %all_to_all.28.own_ref), channel_id=1, source_target_pairs={{0,16},{16,0},{1,17},{17,1},{2,18},{18,2},{3,19},{19,3},{4,20},{20... | collective-permute-start | bytes 983048 | tf_op jit(solution)/shard_map/ppermute | solution.py:270
  148.0 0.7 copy-start.4
Sparse Core Ops, SparseCore 0:
  17.6 106.1 all-gather.1

commit v5 on v4

--- a/solution.py
+++ b/solution.py
@@ -15,6 +15,8 @@
 CHIPS = ("y", "x")
 REPLICAS = ("y", "x", "core")
 CORES_FIRST = ("core", "y", "x")
+SCALARS = pl.BlockSpec(memory_space=pltpu.SMEM)
+VECTORS = pl.BlockSpec(memory_space=pltpu.VMEM)
 
 
 def gelu_tanh(values):
@@ -50,7 +52,7 @@
     )(token_ids.reshape(1, -1), preact, targets)
 
 
-def gram_kernel(blocks_ref, kernel_ref, gram_ref, flat_ref, values_ref):
+def gram_kernel(place_ref, blocks_ref, kernel_ref, kept_ref, sent_ref, flat_ref, values_ref):
     replicas, height, _ = blocks_ref.shape
     rows = kernel_ref.shape[0]
     parts = rows // LANES
@@ -78,31 +80,34 @@
         for own in range(0, products.shape[0], replicas):
             total += products[own : own + replicas, own : own + replicas]
     lines = replicas // 4
-    for half in range(2):
-        first = 2 * half * lines
-        gram_ref[half] = jnp.concatenate(
-            [total[first : first + lines], total[first + lines : first + 2 * lines]], axis=1
-        )
-
-
-def gram(blocks, kernel):
+    quarters = [total[quarter * lines : (quarter + 1) * lines] for quarter in range(4)]
+    upper = jnp.concatenate(quarters[:2], axis=1)
+    lower = jnp.concatenate(quarters[2:], axis=1)
+    first = place_ref[1] == 0
+    kept_ref[...] = jnp.where(first, upper, lower)
+    sent_ref[...] = jnp.where(first, lower, upper)
+
+
+def gram(place, blocks, kernel):
     replicas, height, _ = blocks.shape
     rows = kernel.shape[0]
     return pl.pallas_call(
         gram_kernel,
-        out_shape=jax.ShapeDtypeStruct((2, replicas // 4, 2 * replicas), jnp.float32),
+        in_specs=[SCALARS, VECTORS, VECTORS],
+        out_shape=[jax.ShapeDtypeStruct((replicas // 4, 2 * replicas), jnp.float32)] * 2,
         scratch_shapes=[
             pltpu.VMEM((replicas * height, LANES), jnp.float32),
             pltpu.VMEM((replicas * height * LANES // rows, rows), jnp.bfloat16),
         ],
         name="gram",
-    )(blocks, kernel)
-
-
-def combine_kernel(gram_ref, blocks_ref, sum_ref, weight_ref):
+    )(place, blocks, kernel)
+
+
+def combine_kernel(place_ref, own_ref, other_ref, blocks_ref, sum_ref, weight_ref):
     replicas, height, _ = blocks_ref.shape
-    chips = gram_ref.shape[0] // 2
-    halves = [jnp.sum(gram_ref[half * chips : (half + 1) * chips], axis=0) for half in range(2)]
+    first = place_ref[1] == 0
+    own, other = own_ref[...], other_ref[...]
+    halves = [jnp.where(first, own, other), jnp.where(first, other, own)]
     full = []
     for half in range(2):
         for side in range(2):
@@ -141,14 +146,15 @@
         sum_ref[copy] = total
 
 
-def combine(gram_parts, blocks):
+def combine(place, own, other, blocks):
     replicas, height, _ = blocks.shape
     return pl.pallas_call(
         combine_kernel,
+        in_specs=[SCALARS, VECTORS, VECTORS, VECTORS],
         out_shape=jax.ShapeDtypeStruct((replicas // 2, height, LANES), jnp.bfloat16),
         scratch_shapes=[pltpu.VMEM((LANES, LANES), jnp.float32)],
         name="combine",
-    )(gram_parts, blocks)
+    )(place, own, other, blocks)
 
 
 def exchange(value, axis):
@@ -158,6 +164,27 @@
 def share(value, axis):
     members = lax.axis_size(axis)
     return exchange(jnp.broadcast_to(value, (members, *value.shape)), axis)
+
+
+def swap_cores(value):
+    return lax.ppermute(value, "core", [(0, 1), (1, 0)])
+
+
+def transpose_kernel(table_ref, features_ref):
+    features_ref[...] = table_ref[...].T
+
+
+def transpose(table):
+    rows, features = table.shape
+    block = 640
+    return pl.pallas_call(
+        transpose_kernel,
+        grid=(features // block,),
+        in_specs=[pl.BlockSpec((rows, block), lambda step: (0, step))],
+        out_specs=pl.BlockSpec((block, rows), lambda step: (step, 0)),
+        out_shape=jax.ShapeDtypeStruct((features, rows), table.dtype),
+        name="transpose",
+    )(table)
 
 
 def update_kernel(
@@ -264,12 +291,14 @@
     kernel = lax.dot_general(
         table, table, (((1,), (1,)), ((), ())), preferred_element_type=jnp.float32
     )
-    part = jnp.sum(exchange(gram(blocks, kernel), "core"), axis=0)
-    part = jnp.sum(share(part, "z"), axis=0)
-    own = exchange(combine(share(part, CORES_FIRST), blocks), CHIPS)
-    other = lax.ppermute(own, "core", [(0, 1), (1, 0)])
     place = jnp.stack([lax.axis_index(REPLICAS) * owned_rows, lax.axis_index("core")])
-    return update(place, own, other, table.T, weights, old_momentum, momentum)
+    kept, sent = gram(place, blocks, kernel)
+    part = jnp.sum(share(kept + swap_cores(sent), "z"), axis=0)
+    part = jnp.sum(share(part, CHIPS), axis=0)
+    total = combine(place, part, swap_cores(part), blocks)
+    total, table = lax.optimization_barrier((total, table))
+    own, features = lax.optimization_barrier((exchange(total, CHIPS), transpose(table)))
+    return update(place, own, swap_cores(own), features, weights, old_momentum, momentum)
 
 
 def solution(mesh):

time: 165 us -> 156 us (0.945)
  blocking collectives: 76.9 us -> 40.8 us
  starting transfers between devices: 22.8 us -> 35.3 us
  waiting for transfers between devices: 17.7 us -> 29 us
  Pallas kernels: 18.8 us -> 23.1 us
  local copies, waits for them, and re-layouts: 4.29 us -> 2.22 us
    all_to_all x4 -> x2, blocking collectives: 76.9 us -> 40.8 us  [exchange(): return lax.all_to_all(value, axis, 0, 0, tiled=True)]
    ppermute x1 -> x3, starting transfers between devices: 4.31 us -> 12.9 us  [swap_cores(): return lax.ppermute(value, 'core', [(0, 1), (1, 0)])]
    all_to_all x1 -> x2, waiting for transfers between devices: 17.7 us -> 25.6 us  [exchange(): return lax.all_to_all(value, axis, 0, 0, tiled=True)]
    pallas_call x2 -> x3, Pallas kernels: 6.55 us -> 10.8 us  [the longest x1 4.4 us: transpose(): pl.pallas_call(transpose_kernel, grid=(features // block,), in_specs=[pl....]
    all_to_all x1 -> x2, starting transfers between devices: 18.4 us -> 22.3 us  [exchange(): return lax.all_to_all(value, axis, 0, 0, tiled=True)]
    ppermute x1 -> x3, waiting for transfers between devices: 0.01 us -> 3.39 us  [swap_cores(): return lax.ppermute(value, 'core', [(0, 1), (1, 0)])]
    optimization_barrier x1 -> x0, local copies, waits for them, and re-layouts: 2.65 us -> none  [body(): lax.optimization_barrier((blocks, table, momentum))]
  transfers between devices with their start and end apart: 3 -> 6, of which waited for: 1 -> 5; matrix products, arithmetic and copies ran while one was open for 4% -> 3% of each run, Pallas kernels for 4% -> 7%
where the time goes in v5:
time: 156 us; the launch traced here: 155 us
  blocking collectives  40.8 us (26%)
  starting transfers between devices  35.3 us (23%)
  waiting for transfers between devices  29 us (19%)
  Pallas kernels  23.1 us (15%)
  between operations  14.1 us (9%)
  matrix products  8.25 us (5%)
  local copies, waits for them, and re-layouts  2.22 us (1%)
  other arithmetic  2.03 us (1%)
    all_to_all x2, blocking collectives, exchange(): return lax.all_to_all(value, axis, 0, 0, tiled=True)  40.8 us
    all_to_all x2, waiting for transfers between devices, exchange(): return lax.all_to_all(value, axis, 0, 0, tiled=True)  25.6 us
    all_to_all x2, starting transfers between devices, exchange(): return lax.all_to_all(value, axis, 0, 0, tiled=True)  22.3 us
    ppermute x3, starting transfers between devices, swap_cores(): return lax.ppermute(value, 'core', [(0, 1), (1, 0)])  12.9 us
    pallas_call x1, Pallas kernels, update(): pl.pallas_call(update_kernel, grid_spec=pltpu.PrefetchScalarGridSpec(num_...  8.43 us
    dot_general x1, matrix products, body(): lax.dot_general(weights, table, (((0,), (1,)), ((), ())), preferred_eleme...  5.73 us
    pallas_call x1, Pallas kernels, transpose(): pl.pallas_call(transpose_kernel, grid=(features // block,), in_specs=[pl....  4.4 us
    pallas_call x1, Pallas kernels, row_blocks(): pl.pallas_call(rows_kernel, out_shape=jax.ShapeDtypeStruct((replicas, hei...  3.85 us
  transfers between devices with their start and end apart: 6, of which 5 were waited for; matrix products, arithmetic and copies ran while one was open for 3% of the time, Pallas kernels for 7%

profile of v5, /device:TPU:1, one launch (start us, length us, event | category | flops | bytes accessed | tf_op | source)
XLA Modules:
  0.0 154.8 jit_solution(6718978099476403311)
XLA Ops:
  7.2 0.0 all-gather.2.cloned.1.call-start
  7.2 0.0 copy-start.3
  7.2 5.7 %fusion.preact_ref = f32[640,512]{1,0:T(8,128)} fusion(bf16[2560,640]{1,0:T(8,128)(2,1)} %weights_ref.1, bf16[512,2560]{1,0:T(8,128)(2,1)} %table_ref), kind=kOutput, calls=%fused_computation.1 | convolution fusion | flops 1677721600 | bytes 7208960 | tf_op jit(solution)/shard_map/dot_general | solution.py:284
  12.9 0.0 copy-start.1
  12.9 3.8 %rows.1 = bf16[64,40,128]{2,1,0:T(8,128)(2,1)} custom-call(s32[1,512]{1,0:T(1,128)} %bitcast.7, f32[640,512]{1,0:T(8,128)} %fusion.preact_ref, bf16[512,640]{1,0:T(8,128)(2,1)} %targets_ref.1), custom_call_target="tpu_custom_call" | custom-call | tf_op jit(solution)/shard_map/rows/pallas_call | solution.py:47
  16.8 0.0 copy-done.3
  16.8 0.6 convert_element_type.3
  17.4 0.0 all-gather.2.cloned.1.call-update
  17.5 18.4 %all-to-all-start = ((bf16[64,40,128]{2,1,0:T(8,128)(2,1)}), bf16[64,40,128]{2,1,0:T(8,128)(2,1)S(1)}, u32[]{:S(2)}, u32[]{:S(2)}) async-start(bf16[64,40,128]{2,1,0:T(8,128)(2,1)} %rows.1), calls=%async_computation | async-start | bytes 1310720 | tf_op jit(solution)/shard_map/all_to_all | solution.py:161
  35.9 0.7 pad_add_fusion.place_ref
  36.5 0.0 copy-done.1
  36.5 2.5 %fusion.1.kernel_ref = f32[512,512]{1,0:T(8,128)} fusion(bf16[512,2560]{1,0:T(8,128)(2,1)S(1)} %copy-done.1), kind=kOutput, calls=%fused_computation.2 | convolution fusion | flops 1342177280 | bytes 3670016 | tf_op jit(solution)/shard_map/dot_general | solution.py:291
  39.0 17.1 %all-to-all-done.blocks_ref = bf16[64,40,128]{2,1,0:T(8,128)(2,1)S(1)} async-done(((bf16[64,40,128]{2,1,0:T(8,128)(2,1)}), bf16[64,40,128]{2,1,0:T(8,128)(2,1)S(1)}, u32[]{:S(2)}, u32[]{:S(2)}) %all-to-all-start) | async-done | bytes 655392 | tf_op jit(solution)/shard_map/all_to_all | solution.py:161
  56.1 0.0 copy-start
  56.1 0.8 copy-done
  57.0 3.4 %gram.1 = (f32[16,128]{1,0:T(8,128)}, f32[16,128]{1,0:T(8,128)}) custom-call(s32[2]{0:T(128)} %pad_add_fusion.place_ref, bf16[64,40,128]{2,1,0:T(8,128)(2,1)} %copy-done, f32[512,512]{1,0:T(8,128)} %fusion.1.kernel_ref), custom_call_target="tpu_custom_call" | custom-call | tf_op jit(solution)/shard_map/gram/pallas_call | solution.py:94
  60.3 1.9 %collective-permute-start = (f32[16,128]{1,0:T(8,128)}, f32[16,128]{1,0:T(8,128)S(1)}, u32[]{:S(2)}, u32[]{:S(2)}) collective-permute-start(f32[16,128]{1,0:T(8,128)} %get-tuple-element.14), channel_id=1, source_target_pairs={{0,16},{16,0},{1,17},{17,1},{2,18},{18,2},{3,19},{19,3},{4,20},{20... | collective-permute-start | bytes 24584 | tf_op jit(solution)/shard_map/ppermute | solution.py:170
  62.2 1.3 collective-permute-done
  63.6 0.7 add.11
  64.3 24.0 %all_to_all.20 = f32[16,16,128]{2,1,0:T(8,128)S(1)} all-to-all(f32[16,16,128]{2,1,0:T(8,128)S(1)} %broadcast_in_dim.6), channel_id=1, replica_groups=mesh['y'=8,'x'=4,'core'=2,'z'=16] {'z'}, dimensions={0} | all-to-all | bytes 262144 | tf_op jit(solution)/shard_map/all_to_all | solution.py:161
  88.4 16.8 %all_to_all.21 = f32[32,16,128]{2,1,0:T(8,128)S(1)} all-to-all(f32[32,16,128]{2,1,0:T(8,128)S(1)} %broadcast_in_dim.7), channel_id=1, replica_groups=mesh['y'=8,'x'=4,'core'=2,'z'=16] {'y','x'}, dimensions={0} | all-to-all | bytes 524288 | tf_op jit(solution)/shard_map/all_to_all | solution.py:161
  105.2 0.0 copy-start.5
  105.2 7.0 %collective-permute-start.1 = (f32[16,128]{1,0:T(8,128)S(1)}, f32[16,128]{1,0:T(8,128)S(1)}, u32[]{:S(2)}, u32[]{:S(2)}) collective-permute-start(f32[16,128]{1,0:T(8,128)S(1)} %reduce_sum.19.own_ref), channel_id=1, source_target_pairs={{0,16},{16,0},{1,17},{17,1},{2,18},{18,2},{3,19},{19,3},{4,20},{20... | collective-permute-start | bytes 24584 | tf_op jit(solution)/shard_map/ppermute | solution.py:170
  112.2 0.8 collective-permute-done.1.other_ref
  113.0 0.0 copy-done.5
  113.0 0.0 copy-start.6
  113.0 0.6 copy-done.6
  113.6 3.1 %combine.1 = bf16[32,40,128]{2,1,0:T(8,128)(2,1)} custom-call(s32[2]{0:T(128)} %pad_add_fusion.place_ref, f32[16,128]{1,0:T(8,128)} %copy-done.5, f32[16,128]{1,0:T(8,128)} %copy-done.6, bf16[64,40,128]{2,1,0:T(8,128)(2,1)} %copy-done), custom_call_target="tpu_custom_call" | custom-call | tf_op jit(solution)/shard_map/combine/pallas_call | solution.py:151
  116.7 3.9 %all-to-all-start.3 = ((bf16[32,40,128]{2,1,0:T(8,128)(2,1)}), bf16[32,40,128]{2,1,0:T(8,128)(2,1)S(1)}, u32[]{:S(2)}, u32[]{:S(2)}) async-start(bf16[32,40,128]{2,1,0:T(8,128)(2,1)} %combine.1), calls=%async_computation.3 | async-start | bytes 655360 | tf_op jit(solution)/shard_map/all_to_all | solution.py:161
  120.5 4.4 %transpose.1.features_ref = bf16[2560,512]{1,0:T(8,128)(2,1)} custom-call(bf16[512,2560]{1,0:T(8,128)(2,1)} %table_ref), custom_call_target="tpu_custom_call" | custom-call | tf_op jit(solution)/shard_map/transpose/pallas_call | solution.py:180
  124.9 8.6 %all-to-all-done.3.own_ref = bf16[32,40,128]{2,1,0:T(8,128)(2,1)S(1)} async-done(((bf16[32,40,128]{2,1,0:T(8,128)(2,1)}), bf16[32,40,128]{2,1,0:T(8,128)(2,1)S(1)}, u32[]{:S(2)}, u32[]{:S(2)}) %all-to-all-start.3) | async-done | bytes 327712 | tf_op jit(solution)/shard_map/all_to_all | solution.py:161
  133.5 0.0 copy-start.2
  133.5 4.1 %collective-permute-start.2 = (bf16[32,40,128]{2,1,0:T(8,128)(2,1)S(1)}, bf16[32,40,128]{2,1,0:T(8,128)(2,1)S(1)}, u32[]{:S(2)}, u32[]{:S(2)}) collective-permute-start(bf16[32,40,128]{2,1,0:T(8,128)(2,1)S(1)} %all-to-all-done.3.own_ref), channel_id=1, source_target_pairs={{0,16},{16,0},{1,17},{17,1},{2,18},{18,2},{3,19},{19,3},{4,20},{20... | collective-permute-start | bytes 983048 | tf_op jit(solution)/shard_map/ppermute | solution.py:170
  137.6 1.2 collective-permute-done.2.other_ref
  138.8 0.0 copy-start.4
  138.8 0.0 all-gather.2.cloned.1.call-done.old_ref
  138.8 0.0 copy-done.2
  138.8 0.7 copy-done.4
  139.6 8.4 %update.1 = (bf16[2560,640]{1,0:T(8,128)(2,1)}, f32[40,640]{1,0:T(8,128)}) custom-call(s32[2]{0:T(128)} %pad_add_fusion.place_ref, bf16[32,40,128]{2,1,0:T(8,128)(2,1)} %copy-done.2, bf16[32,40,128]{2,1,0:T(8,128)(2,1)} %copy-done.4, bf16[2560,512]{1,0:T(8,128)(2,1)} %transpose.1.features_ref, bf16[2560,640]{1,0:T(8,128)(2,1)} %weights_ref.1, ...), custom_call_target="tpu_custom_call" | custom-call | tf_op jit(solution)/shard_map/update/pallas_call | solution.py:245
  (4 shorter events, 0.1 us)
Async XLA Ops:
  7.2 131.7 %all-gather.2.cloned.1.call-start = ((), (), s32[]{:S(2)}) async-start(), calls=%async_computation.4 | async-start | bytes 3328000 | tf_op jit(solution)/shard_map/all_gather | solution.py:289
  7.2 9.6 %copy-start.3 = (f32[40,640]{1,0:T(8,128)S(1)}, f32[40,640]{1,0:T(8,128)}, u32[]{:S(2)}) copy-start(f32[40,640]{1,0:T(8,128)} %momentum_ref) | copy-start | bytes 307204
  12.9 23.6 %copy-start.1 = (bf16[512,2560]{1,0:T(8,128)(2,1)S(1)}, bf16[512,2560]{1,0:T(8,128)(2,1)}, u32[]{:S(2)}) copy-start(bf16[512,2560]{1,0:T(8,128)(2,1)} %table_ref) | copy-start | bytes 7864324
  17.5 38.7 %all-to-all-start = ((bf16[64,40,128]{2,1,0:T(8,128)(2,1)}), bf16[64,40,128]{2,1,0:T(8,128)(2,1)S(1)}, u32[]{:S(2)}, u32[]{:S(2)}) async-start(bf16[64,40,128]{2,1,0:T(8,128)(2,1)} %rows.1), calls=%async_computation | async-start | bytes 1310720 | tf_op jit(solution)/shard_map/all_to_all | solution.py:161
  56.1 0.8 copy-start
  60.3 3.3 %collective-permute-start = (f32[16,128]{1,0:T(8,128)}, f32[16,128]{1,0:T(8,128)S(1)}, u32[]{:S(2)}, u32[]{:S(2)}) collective-permute-start(f32[16,128]{1,0:T(8,128)} %get-tuple-element.14), channel_id=1, source_target_pairs={{0,16},{16,0},{1,17},{17,1},{2,18},{18,2},{3,19},{19,3},{4,20},{20... | collective-permute-start | bytes 24584 | tf_op jit(solution)/shard_map/ppermute | solution.py:170
  105.2 7.8 %copy-start.5 = (f32[16,128]{1,0:T(8,128)}, f32[16,128]{1,0:T(8,128)S(1)}, u32[]{:S(2)}) copy-start(f32[16,128]{1,0:T(8,128)S(1)} %reduce_sum.19.own_ref) | copy-start | bytes 24580
  105.2 7.8 %collective-permute-start.1 = (f32[16,128]{1,0:T(8,128)S(1)}, f32[16,128]{1,0:T(8,128)S(1)}, u32[]{:S(2)}, u32[]{:S(2)}) collective-permute-start(f32[16,128]{1,0:T(8,128)S(1)} %reduce_sum.19.own_ref), channel_id=1, source_target_pairs={{0,16},{16,0},{1,17},{17,1},{2,18},{18,2},{3,19},{19,3},{4,20},{20... | collective-permute-start | bytes 24584 | tf_op jit(solution)/shard_map/ppermute | solution.py:170
  113.0 0.6 copy-start.6
  116.7 16.9 %all-to-all-start.3 = ((bf16[32,40,128]{2,1,0:T(8,128)(2,1)}), bf16[32,40,128]{2,1,0:T(8,128)(2,1)S(1)}, u32[]{:S(2)}, u32[]{:S(2)}) async-start(bf16[32,40,128]{2,1,0:T(8,128)(2,1)} %combine.1), calls=%async_computation.3 | async-start | bytes 655360 | tf_op jit(solution)/shard_map/all_to_all | solution.py:161
  133.5 5.3 %copy-start.2 = (bf16[32,40,128]{2,1,0:T(8,128)(2,1)}, bf16[32,40,128]{2,1,0:T(8,128)(2,1)S(1)}, u32[]{:S(2)}) copy-start(bf16[32,40,128]{2,1,0:T(8,128)(2,1)S(1)} %all-to-all-done.3.own_ref) | copy-start | bytes 983044
  133.5 5.3 %collective-permute-start.2 = (bf16[32,40,128]{2,1,0:T(8,128)(2,1)S(1)}, bf16[32,40,128]{2,1,0:T(8,128)(2,1)S(1)}, u32[]{:S(2)}, u32[]{:S(2)}) collective-permute-start(bf16[32,40,128]{2,1,0:T(8,128)(2,1)S(1)} %all-to-all-done.3.own_ref), channel_id=1, source_target_pairs={{0,16},{16,0},{1,17},{17,1},{2,18},{18,2},{3,19},{19,3},{4,20},{20... | collective-permute-start | bytes 983048 | tf_op jit(solution)/shard_map/ppermute | solution.py:170
  138.8 0.7 copy-start.4
Sparse Core Ops, SparseCore 0:
  17.6 103.6 all-gather.1

commit v6 on v5

--- a/solution.py
+++ b/solution.py
@@ -15,6 +15,7 @@
 CHIPS = ("y", "x")
 REPLICAS = ("y", "x", "core")
 CORES_FIRST = ("core", "y", "x")
+SMALL = pltpu.CompilerParams(vmem_limit_bytes=24 * 2**20)
 SCALARS = pl.BlockSpec(memory_space=pltpu.SMEM)
 VECTORS = pl.BlockSpec(memory_space=pltpu.VMEM)
 
@@ -48,6 +49,7 @@
         rows_kernel,
         out_shape=jax.ShapeDtypeStruct((replicas, height // replicas, LANES), jnp.bfloat16),
         scratch_shapes=[pltpu.VMEM((height, LANES), jnp.float32)],
+        compiler_params=SMALL,
         name="rows",
     )(token_ids.reshape(1, -1), preact, targets)
 
@@ -99,6 +101,7 @@
             pltpu.VMEM((replicas * height, LANES), jnp.float32),
             pltpu.VMEM((replicas * height * LANES // rows, rows), jnp.bfloat16),
         ],
+        compiler_params=SMALL,
         name="gram",
     )(place, blocks, kernel)
 
@@ -153,6 +156,7 @@
         in_specs=[SCALARS, VECTORS, VECTORS, VECTORS],
         out_shape=jax.ShapeDtypeStruct((replicas // 2, height, LANES), jnp.bfloat16),
         scratch_shapes=[pltpu.VMEM((LANES, LANES), jnp.float32)],
+        compiler_params=SMALL,
         name="combine",
     )(place, own, other, blocks)
 

time: 156 us -> 148 us (0.949)
  Pallas kernels: 23.1 us -> 19.4 us
    pallas_call x1, Pallas kernels: 3.85 us -> 2.17 us  [row_blocks(): pl.pallas_call(rows_kernel, out_shape=jax.ShapeDtypeStruct((replicas, hei...]
  transfers between devices with their start and end apart: 6 -> 6, of which waited for: 5 -> 5; matrix products, arithmetic and copies ran while one was open for 3% -> 3% of each run, Pallas kernels for 7% -> 6%
where the time goes in v6:
time: 148 us
  blocking collectives  40.9 us (28%)
  starting transfers between devices  35.3 us (24%)
  waiting for transfers between devices  27.7 us (19%)
  Pallas kernels  19.4 us (13%)
  between operations  14.2 us (10%)
  matrix products  8.76 us (6%)
    all_to_all x2, blocking collectives, exchange(): return lax.all_to_all(value, axis, 0, 0, tiled=True)  40.9 us
    all_to_all x2, waiting for transfers between devices, exchange(): return lax.all_to_all(value, axis, 0, 0, tiled=True)  24.5 us
    all_to_all x2, starting transfers between devices, exchange(): return lax.all_to_all(value, axis, 0, 0, tiled=True)  22.3 us
    ppermute x3, starting transfers between devices, swap_cores(): return lax.ppermute(value, 'core', [(0, 1), (1, 0)])  13 us
    pallas_call x1, Pallas kernels, update(): pl.pallas_call(update_kernel, grid_spec=pltpu.PrefetchScalarGridSpec(num_...  8.43 us
    dot_general x1, matrix products, body(): lax.dot_general(weights, table, (((0,), (1,)), ((), ())), preferred_eleme...  4.69 us
    pallas_call x1, Pallas kernels, transpose(): pl.pallas_call(transpose_kernel, grid=(features // block,), in_specs=[pl....  4.43 us
    dot_general x1, matrix products, body(): lax.dot_general(table, table, (((1,), (1,)), ((), ())), preferred_element...  4.07 us
  transfers between devices with their start and end apart: 6, of which 5 were waited for; matrix products, arithmetic and copies ran while one was open for 3% of the time, Pallas kernels for 6%

profile of v6, /device:TPU:1, one launch (start us, length us, event | category | flops | bytes accessed | tf_op | source)
XLA Modules:
  0.0 147.7 jit_solution(12100540623595494258)
XLA Ops:
  7.2 0.0 copy-start
  7.2 0.0 copy-start.2
  7.2 0.0 all-gather.2.cloned.1.call-start
  7.2 4.7 %fusion.preact_ref = f32[640,512]{1,0:T(8,128)S(1)} fusion(bf16[2560,640]{1,0:T(8,128)(2,1)} %weights_ref.1, bf16[512,2560]{1,0:T(8,128)(2,1)} %table_ref), kind=kOutput, calls=%fused_computation.1 | convolution fusion | flops 1677721600 | bytes 7208960 | tf_op jit(solution)/shard_map/dot_general | solution.py:288
  11.9 0.0 copy-start.4
  11.9 0.0 copy-done
  11.9 0.0 copy-done.2
  12.0 2.2 %rows.1 = bf16[64,40,128]{2,1,0:T(8,128)(2,1)} custom-call(s32[1,512]{1,0:T(1,128)S(1)} %bitcast.7, f32[640,512]{1,0:T(8,128)S(1)} %fusion.preact_ref, bf16[512,640]{1,0:T(8,128)(2,1)S(1)} %copy-done), custom_call_target="tpu_custom_call" | custom-call | tf_op jit(solution)/shard_map/rows/pallas_call | solution.py:48
  14.1 0.0 copy-done.4
  14.1 0.6 convert_element_type.3
  14.8 0.0 all-gather.2.cloned.1.call-update
  14.8 18.4 %all-to-all-start = ((bf16[64,40,128]{2,1,0:T(8,128)(2,1)}), bf16[64,40,128]{2,1,0:T(8,128)(2,1)S(1)}, u32[]{:S(2)}, u32[]{:S(2)}) async-start(bf16[64,40,128]{2,1,0:T(8,128)(2,1)} %rows.1), calls=%async_computation | async-start | bytes 1310720 | tf_op jit(solution)/shard_map/all_to_all | solution.py:165
  33.2 0.1 pad_add_fusion.place_ref
  33.3 0.0 copy-start.1
  33.3 4.1 %fusion.1.kernel_ref = f32[512,512]{1,0:T(8,128)S(1)} fusion(bf16[512,2560]{1,0:T(8,128)(2,1)} %table_ref), kind=kOutput, calls=%fused_computation.2 | convolution fusion | flops 1342177280 | bytes 3670016 | tf_op jit(solution)/shard_map/dot_general | solution.py:295
  37.4 16.1 %all-to-all-done.blocks_ref = bf16[64,40,128]{2,1,0:T(8,128)(2,1)S(1)} async-done(((bf16[64,40,128]{2,1,0:T(8,128)(2,1)}), bf16[64,40,128]{2,1,0:T(8,128)(2,1)S(1)}, u32[]{:S(2)}, u32[]{:S(2)}) %all-to-all-start) | async-done | bytes 655392 | tf_op jit(solution)/shard_map/all_to_all | solution.py:165
  53.4 1.9 %gram.1 = (f32[16,128]{1,0:T(8,128)S(1)}, f32[16,128]{1,0:T(8,128)S(1)}) custom-call(s32[2]{0:T(128)S(1)} %pad_add_fusion.place_ref, bf16[64,40,128]{2,1,0:T(8,128)(2,1)S(1)} %all-to-all-done.blocks_ref, f32[512,512]{1,0:T(8,128)S(1)} %fusion.1.kernel_ref), custom_call_target="tpu_custom_call" | custom-call | tf_op jit(solution)/shard_map/gram/pallas_call | solution.py:96
  55.3 1.9 %collective-permute-start = (f32[16,128]{1,0:T(8,128)S(1)}, f32[16,128]{1,0:T(8,128)S(1)}, u32[]{:S(2)}, u32[]{:S(2)}) collective-permute-start(f32[16,128]{1,0:T(8,128)S(1)} %get-tuple-element.14), channel_id=1, source_target_pairs={{0,16},{16,0},{1,17},{17,1},{2,18},{18,2},{3,19},{19,3},{4,20},{20... | collective-permute-start | bytes 24584 | tf_op jit(solution)/shard_map/ppermute | solution.py:174
  57.2 1.1 collective-permute-done
  58.4 24.0 %all_to_all.20 = f32[16,16,128]{2,1,0:T(8,128)S(1)} all-to-all(f32[16,16,128]{2,1,0:T(8,128)S(1)} %broadcast_in_dim.6), channel_id=1, replica_groups=mesh['y'=8,'x'=4,'core'=2,'z'=16] {'z'}, dimensions={0} | all-to-all | bytes 262144 | tf_op jit(solution)/shard_map/all_to_all | solution.py:165
  82.5 16.9 %all_to_all.21 = f32[32,16,128]{2,1,0:T(8,128)S(1)} all-to-all(f32[32,16,128]{2,1,0:T(8,128)S(1)} %broadcast_in_dim.7), channel_id=1, replica_groups=mesh['y'=8,'x'=4,'core'=2,'z'=16] {'y','x'}, dimensions={0} | all-to-all | bytes 524288 | tf_op jit(solution)/shard_map/all_to_all | solution.py:165
  99.4 6.9 %collective-permute-start.1 = (f32[16,128]{1,0:T(8,128)S(1)}, f32[16,128]{1,0:T(8,128)S(1)}, u32[]{:S(2)}, u32[]{:S(2)}) collective-permute-start(f32[16,128]{1,0:T(8,128)S(1)} %reduce_sum.19.own_ref), channel_id=1, source_target_pairs={{0,16},{16,0},{1,17},{17,1},{2,18},{18,2},{3,19},{19,3},{4,20},{20... | collective-permute-start | bytes 24584 | tf_op jit(solution)/shard_map/ppermute | solution.py:174
  106.3 0.8 collective-permute-done.1.other_ref
  107.1 0.0 copy-done.1
  107.1 2.5 %combine.1 = bf16[32,40,128]{2,1,0:T(8,128)(2,1)} custom-call(s32[2]{0:T(128)S(1)} %pad_add_fusion.place_ref, f32[16,128]{1,0:T(8,128)S(1)} %reduce_sum.19.own_ref, f32[16,128]{1,0:T(8,128)S(1)} %collective-permute-done.1.other_ref, bf16[64,40,128]{2,1,0:T(8,128)(2,1)S(1)} %all-to-all-done.blocks_ref), custom_call_target="tpu_custom_call" | custom-call | tf_op jit(solution)/shard_map/combine/pallas_call | solution.py:154
  109.5 3.9 %all-to-all-start.3 = ((bf16[32,40,128]{2,1,0:T(8,128)(2,1)}), bf16[32,40,128]{2,1,0:T(8,128)(2,1)S(1)}, u32[]{:S(2)}, u32[]{:S(2)}) async-start(bf16[32,40,128]{2,1,0:T(8,128)(2,1)} %combine.1), calls=%async_computation.3 | async-start | bytes 655360 | tf_op jit(solution)/shard_map/all_to_all | solution.py:165
  113.4 4.4 %transpose.1.features_ref = bf16[2560,512]{1,0:T(8,128)(2,1)} custom-call(bf16[512,2560]{1,0:T(8,128)(2,1)} %table_ref), custom_call_target="tpu_custom_call" | custom-call | tf_op jit(solution)/shard_map/transpose/pallas_call | solution.py:184
  117.9 8.4 %all-to-all-done.3.own_ref = bf16[32,40,128]{2,1,0:T(8,128)(2,1)S(1)} async-done(((bf16[32,40,128]{2,1,0:T(8,128)(2,1)}), bf16[32,40,128]{2,1,0:T(8,128)(2,1)S(1)}, u32[]{:S(2)}, u32[]{:S(2)}) %all-to-all-start.3) | async-done | bytes 327712 | tf_op jit(solution)/shard_map/all_to_all | solution.py:165
  126.3 0.0 copy-start.3
  126.3 4.2 %collective-permute-start.2 = (bf16[32,40,128]{2,1,0:T(8,128)(2,1)S(1)}, bf16[32,40,128]{2,1,0:T(8,128)(2,1)S(1)}, u32[]{:S(2)}, u32[]{:S(2)}) collective-permute-start(bf16[32,40,128]{2,1,0:T(8,128)(2,1)S(1)} %all-to-all-done.3.own_ref), channel_id=1, source_target_pairs={{0,16},{16,0},{1,17},{17,1},{2,18},{18,2},{3,19},{19,3},{4,20},{20... | collective-permute-start | bytes 983048 | tf_op jit(solution)/shard_map/ppermute | solution.py:174
  130.5 1.2 collective-permute-done.2.other_ref
  131.7 0.0 copy-start.5
  131.7 0.0 all-gather.2.cloned.1.call-done.old_ref
  131.7 0.0 copy-done.3
  131.7 0.7 copy-done.5
  132.4 8.4 %update.1 = (bf16[2560,640]{1,0:T(8,128)(2,1)}, f32[40,640]{1,0:T(8,128)}) custom-call(s32[2]{0:T(128)} %copy-done.1, bf16[32,40,128]{2,1,0:T(8,128)(2,1)} %copy-done.3, bf16[32,40,128]{2,1,0:T(8,128)(2,1)} %copy-done.5, bf16[2560,512]{1,0:T(8,128)(2,1)} %transpose.1.features_ref, bf16[2560,640]{1,0:T(8,128)(2,1)} %weights_ref.1, ...), custom_call_target="tpu_custom_call" | custom-call | tf_op jit(solution)/shard_map/update/pallas_call | solution.py:249
  (5 shorter events, 0.1 us)
Async XLA Ops:
  7.2 4.8 %copy-start = (bf16[512,640]{1,0:T(8,128)(2,1)S(1)}, bf16[512,640]{1,0:T(8,128)(2,1)}, u32[]{:S(2)}) copy-start(bf16[512,640]{1,0:T(8,128)(2,1)} %targets_ref.1) | copy-start | bytes 1966084
  7.2 4.8 %copy-start.2 = (s32[512]{0:T(512)S(1)}, s32[512]{0:T(512)}, u32[]{:S(2)}) copy-start(s32[512]{0:T(512)} %param.5) | copy-start | bytes 6148
  7.2 124.5 %all-gather.2.cloned.1.call-start = ((), (), s32[]{:S(2)}) async-start(), calls=%async_computation.4 | async-start | bytes 3328000 | tf_op jit(solution)/shard_map/all_gather | solution.py:293
  11.9 2.2 %copy-start.4 = (f32[40,640]{1,0:T(8,128)S(1)}, f32[40,640]{1,0:T(8,128)}, u32[]{:S(2)}) copy-start(f32[40,640]{1,0:T(8,128)} %momentum_ref) | copy-start | bytes 307204
  14.8 38.7 %all-to-all-start = ((bf16[64,40,128]{2,1,0:T(8,128)(2,1)}), bf16[64,40,128]{2,1,0:T(8,128)(2,1)S(1)}, u32[]{:S(2)}, u32[]{:S(2)}) async-start(bf16[64,40,128]{2,1,0:T(8,128)(2,1)} %rows.1), calls=%async_computation | async-start | bytes 1310720 | tf_op jit(solution)/shard_map/all_to_all | solution.py:165
  33.3 73.8 %copy-start.1 = (s32[2]{0:T(128)}, s32[2]{0:T(128)S(1)}, u32[]{:S(2)}) copy-start(s32[2]{0:T(128)S(1)} %pad_add_fusion.place_ref) | copy-start | bytes 28
  55.3 3.1 %collective-permute-start = (f32[16,128]{1,0:T(8,128)S(1)}, f32[16,128]{1,0:T(8,128)S(1)}, u32[]{:S(2)}, u32[]{:S(2)}) collective-permute-start(f32[16,128]{1,0:T(8,128)S(1)} %get-tuple-element.14), channel_id=1, source_target_pairs={{0,16},{16,0},{1,17},{17,1},{2,18},{18,2},{3,19},{19,3},{4,20},{20... | collective-permute-start | bytes 24584 | tf_op jit(solution)/shard_map/ppermute | solution.py:174
  99.4 7.7 %collective-permute-start.1 = (f32[16,128]{1,0:T(8,128)S(1)}, f32[16,128]{1,0:T(8,128)S(1)}, u32[]{:S(2)}, u32[]{:S(2)}) collective-permute-start(f32[16,128]{1,0:T(8,128)S(1)} %reduce_sum.19.own_ref), channel_id=1, source_target_pairs={{0,16},{16,0},{1,17},{17,1},{2,18},{18,2},{3,19},{19,3},{4,20},{20... | collective-permute-start | bytes 24584 | tf_op jit(solution)/shard_map/ppermute | solution.py:174
  109.5 16.7 %all-to-all-start.3 = ((bf16[32,40,128]{2,1,0:T(8,128)(2,1)}), bf16[32,40,128]{2,1,0:T(8,128)(2,1)S(1)}, u32[]{:S(2)}, u32[]{:S(2)}) async-start(bf16[32,40,128]{2,1,0:T(8,128)(2,1)} %combine.1), calls=%async_computation.3 | async-start | bytes 655360 | tf_op jit(solution)/shard_map/all_to_all | solution.py:165
  126.3 5.4 %copy-start.3 = (bf16[32,40,128]{2,1,0:T(8,128)(2,1)}, bf16[32,40,128]{2,1,0:T(8,128)(2,1)S(1)}, u32[]{:S(2)}) copy-start(bf16[32,40,128]{2,1,0:T(8,128)(2,1)S(1)} %all-to-all-done.3.own_ref) | copy-start | bytes 983044
  126.3 5.4 %collective-permute-start.2 = (bf16[32,40,128]{2,1,0:T(8,128)(2,1)S(1)}, bf16[32,40,128]{2,1,0:T(8,128)(2,1)S(1)}, u32[]{:S(2)}, u32[]{:S(2)}) collective-permute-start(bf16[32,40,128]{2,1,0:T(8,128)(2,1)S(1)} %all-to-all-done.3.own_ref), channel_id=1, source_target_pairs={{0,16},{16,0},{1,17},{17,1},{2,18},{18,2},{3,19},{19,3},{4,20},{20... | collective-permute-start | bytes 983048 | tf_op jit(solution)/shard_map/ppermute | solution.py:174
  131.7 0.7 copy-start.5
Sparse Core Ops, SparseCore 0:
  14.9 103.8 all-gather.1
